TPU v7x, 256 devices: a whole 4x4x8 slice. The times are simulated.
256 devices in a mesh: af: 64 (over y_hi, z, x), row: 4 (over y_lo, core).
Axes of the slice: x: 4, y: 4 (y_hi: 2, y_lo: 2; y = y_hi * 2 + y_lo), z: 8, core: 2. Of those that a mesh axis runs over, the one named last changes fastest.
Arguments:
- source_traces: bfloat16 [512, 1024, 2048], P('af', 'row'), may hold values from -6 to 6
- receiver_traces: bfloat16 [128, 1024, 2048], P('row', 'af'), may hold values from -6 to 6
- wavelet_inverse: float32 [64, 2], replicated, may hold values from -4 to 4
Outputs:
- multiples: bfloat16 [512, 128, 2048], P('af', 'row')
All inputs are finite; a program needn't handle non-finite values.
Results may differ from a plain program's by a relative error of at most 0.008.
Values may be sent and summed in bfloat16 or wider, within the bound.
No kernel may reach another device: no remote copies, remote signals or barrier semaphores. Data moves between devices by JAX's collectives and lax.ppermute only.
A program may use at most 64 MiB of HBM per device.

v0:
```python
import math

import jax
import jax.numpy as jnp
from jax import lax
from jax.sharding import PartitionSpec as P

NT = 2048
NF = 64
F_LOW = 96
K = 1024


def tables(amplitude):
    samples = jnp.arange(NT, dtype=jnp.int32)
    frequency = F_LOW + jnp.arange(NF, dtype=jnp.int32)
    phase_index = frequency[:, None] * samples[None, :] % NT
    angles = phase_index.astype(jnp.float32) * (2.0 * math.pi / NT)
    return jnp.stack([jnp.cos(angles) * amplitude, -jnp.sin(angles) * amplitude], axis=1).astype(
        jnp.bfloat16
    )


def coupling(recv_block):
    rcv_real = recv_block[:, 0]
    rcv_imag = recv_block[:, 1]
    real_row = jnp.stack([rcv_real, -rcv_imag], axis=1)
    imag_row = jnp.stack([rcv_imag, rcv_real], axis=1)
    return jnp.stack([real_row, imag_row], axis=1)


def per_device(source_traces, receiver_traces, wavelet_inverse):
    forward = tables(1.0 / math.sqrt(NT))
    source_spec = jnp.einsum(
        "fct,skt->fcsk", forward, source_traces, preferred_element_type=jnp.float32
    ).astype(jnp.bfloat16)
    receiver_spec = jnp.einsum(
        "fct,rkt->fckr", forward, receiver_traces, preferred_element_type=jnp.float32
    ).astype(jnp.bfloat16)
    source_freq, receiver_freq = (
        lax.all_to_all(source_spec, "af", split_axis=0, concat_axis=2, tiled=True),
        lax.all_to_all(receiver_spec, "af", split_axis=0, concat_axis=2, tiled=True),
    )
    local_freqs = source_freq.shape[0]
    raw = jnp.einsum(
        "fockr,fcsk->rfos",
        coupling(receiver_freq),
        lax.all_gather(source_freq, "row", axis=3, tiled=True),
        preferred_element_type=jnp.float32,
    )
    first_freq = lax.axis_index("af") * local_freqs
    wavelet_rows = lax.dynamic_slice_in_dim(wavelet_inverse, first_freq, local_freqs, 0)
    wave_real = wavelet_rows[:, 0][None, :, None]
    wave_imag = wavelet_rows[:, 1][None, :, None]
    raw_real = raw[:, :, 0, :]
    raw_imag = raw[:, :, 1, :]
    amplitude = 1.0 / math.sqrt(K)
    pred_real = (raw_real * wave_real - raw_imag * wave_imag) * amplitude
    pred_imag = (raw_real * wave_imag + raw_imag * wave_real) * amplitude
    predicted = jnp.stack([pred_real, pred_imag], axis=2).astype(jnp.bfloat16)
    returned = lax.all_to_all(predicted, "af", split_axis=3, concat_axis=1, tiled=True)
    inverse = tables(1.0 / math.sqrt(NF))
    result = jnp.einsum("rfcs,fct->srt", returned, inverse, preferred_element_type=jnp.float32)
    return result.astype(jnp.bfloat16)


def solution(mesh):
    return jax.shard_map(
        per_device,
        mesh=mesh,
        in_specs=(P("af", "row", None), P("row", "af", None), P()),
        out_specs=P("af", "row", None),
        check_vma=False,
    )
```

profile of v0, /device:TPU:1, one launch (start us, length us, event | category | flops | bytes accessed | tf_op | source)
XLA Modules:
  0.0 115.3 jit_solution(388761204805325706)
XLA Ops:
  6.5 2.5 %multiply_convert_fusion.1 = (bf16[64,1,2048]{2,0,1:T(8,128)(2,1)S(1)}, bf16[64,1,2048]{2,0,1:T(8,128)(2,1)S(1)}, bf16[64,1,2048]{2,0,1:T(8,128)(2,1)S(1)}, bf16[64,1,2048]{2,0,1:T(8,128)(2,1)S(1)}) fusion(s32[64]{0:T(128)S(1)} %iota_add_fusion), kind=kLoop, calls=%fused_computation.26 | loop fusion | flops 3014656 | bytes 1048832 | tf_op jit(solution)/shard_map/convert.2
  9.1 6.3 %fusion.9 = bf16[64,2,8,256]{3,0,2,1:T(8,128)(2,1)S(1)} fusion(bf16[8,256,2048]{2,1,0:T(8,128)(2,1)} %param.3, bf16[64,1,2048]{2,0,1:T(8,128)(2,1)S(1)} %get-tuple-element.15, bf16[64,1,2048]{2,0,1:T(8,128)(2,1)S(1)} %get-tuple-element.13), kind=kOutput, calls=%fused_computation.10 | convolution fusion | flops 1075052544 | bytes 9437184 | tf_op jit(solution)/shard_map/fct,skt->fcsk/dot_general | solution.py:34
  15.3 0.3 copy.13
  15.6 32.5 %all_to_all.54 = bf16[64,2,8,256]{3,2,1,0:T(8,128)(2,1)S(1)} all-to-all(bf16[64,2,8,256]{3,2,1,0:T(8,128)(2,1)S(1)} %copy.13), channel_id=1, replica_groups=mesh['af'=64,'row'=4] {'af'}, dimensions={0} | all-to-all | bytes 1048576 | tf_op jit(solution)/shard_map/all_to_all | solution.py:41
  48.1 0.8 copy.39
  49.0 1.5 %fusion.15 = bf16[64,2,16,32]{0,3,2,1:T(8,128)(2,1)S(1)} fusion(bf16[32,16,2048]{2,1,0:T(8,128)(2,1)S(1)} %copy-done.1, bf16[64,1,2048]{2,0,1:T(8,128)(2,1)S(1)} %get-tuple-element.15, bf16[64,1,2048]{2,0,1:T(8,128)(2,1)S(1)} %get-tuple-element.13), kind=kOutput, calls=%fused_computation.12 | convolution fusion | flops 269549568 | bytes 2752512 | tf_op jit(solution)/shard_map/fct,rkt->fckr/dot_general | solution.py:37
  50.5 0.8 copy.16
  51.3 1.1 reshape.223
  52.4 6.9 %all-to-all-start.1 = ((bf16[64,2,512]{2,1,0:T(2,128)(2,1)}), bf16[64,2,512]{2,1,0:T(2,128)(2,1)S(1)}, u32[]{:S(2)}, u32[]{:S(2)}) async-start(bf16[64,2,512]{2,1,0:T(2,128)(2,1)} %reshape.223), calls=%async_computation.1 | async-start | bytes 262144 | tf_op jit(solution)/shard_map/all_to_all | solution.py:42
  59.3 0.1 constant_dynamic-slice_fusion
  59.4 0.6 fusion.38
  60.0 10.8 %all-to-all-done.1 = bf16[64,2,512]{2,1,0:T(2,128)(2,1)S(1)} async-done(((bf16[64,2,512]{2,1,0:T(2,128)(2,1)}), bf16[64,2,512]{2,1,0:T(2,128)(2,1)S(1)}, u32[]{:S(2)}, u32[]{:S(2)}) %all-to-all-start.1) | async-done | bytes 131104 | tf_op jit(solution)/shard_map/all_to_all | solution.py:42
  70.8 0.3 reshape.224
  71.2 0.1 copy.29
  71.3 0.1 copy.28
  71.5 7.5 %all-gather.2.cloned.1.call-done = bf16[1,2,512,1024]{3,2,1,0:T(8,128)(2,1)} async-done(((bf16[1,2,512,256]{3,2,1,0:T(8,128)(2,1)}), bf16[1,2,512,1024]{3,2,1,0:T(8,128)(2,1)}) %all-gather.2.cloned.1.call-update) | async-done | bytes 2097168 | tf_op jit(solution)/shard_map/all_gather | solution.py:48
  79.0 2.4 %fusion.18 = f32[32,1,2,512]{3,0,2,1:T(8,128)S(1)} fusion(bf16[1,2,512,1024]{3,2,1,0:T(8,128)(2,1)} %all-gather.2.cloned.1.call-done, bf16[1,1,2,1024,32]{3,4,2,1,0:T(8,128)(2,1)S(1)} %get-tuple-element.10, bf16[1,1,2,1024,32]{3,4,2,1,0:T(8,128)(2,1)S(1)} %get-tuple-element.9), kind=kOutput, calls=%fused_computation.13 | convolution fusion | flops 134742016 | bytes 2490368 | tf_op jit(solution)/shard_map/fockr,fcsk->rfos/dot_general | solution.py:45
  81.4 1.3 %multiply_convert_fusion.5 = (bf16[32,1,1,512]{3,0,2,1:T(8,128)(2,1)S(1)}, bf16[32,1,1,512]{3,0,2,1:T(8,128)(2,1)S(1)}) fusion(f32[32,1,2,512]{3,0,2,1:T(8,128)S(1)} %fusion.18, f32[]{:T(128)} %bitcast.24, f32[]{:T(128)} %bitcast.22), kind=kLoop, calls=%fused_computation.42 | loop fusion | flops 163840 | bytes 196616 | tf_op jit(solution)/shard_map/convert
  82.6 0.2 copy.20
  82.8 0.2 reshape.225
  83.0 23.5 %all_to_all.55 = bf16[64,2,256]{2,1,0:T(2,128)(2,1)S(1)} all-to-all(bf16[64,2,256]{2,1,0:T(2,128)(2,1)S(1)} %reshape.225), channel_id=1, replica_groups=mesh['af'=64,'row'=4] {'af'}, dimensions={0} | all-to-all | bytes 131072 | tf_op jit(solution)/shard_map/all_to_all | solution.py:61
  106.5 0.2 reshape.226
  106.7 0.3 copy.22
  107.0 1.4 %fusion.3 = bf16[8,32,2048]{2,1,0:T(8,128)(2,1)} fusion(bf16[64,1,2048]{2,0,1:T(8,128)(2,1)S(1)} %get-tuple-element.14, bf16[64,1,2048]{2,0,1:T(8,128)(2,1)S(1)} %get-tuple-element.16, bf16[32,1,2,64,8]{3,0,2,4,1:T(8,128)(2,1)S(1)} %copy.22), kind=kOutput, calls=%fused_computation.4 | convolution fusion | flops 135790592 | bytes 1638400 | tf_op jit(solution)/shard_map/rfcs,fct->srt/dot_general | solution.py:63
  (12 shorter events, 0.2 us)
Async XLA Ops:
  6.5 52.8 %copy-start = (f32[64,2]{0,1:T(2,128)S(1)}, f32[64,2]{0,1:T(2,128)}, u32[]{:S(2)}) copy-start(f32[64,2]{0,1:T(2,128)} %param.5) | copy-start | bytes 1540
  6.5 72.5 %all-gather.2.cloned.1.call-start = ((), (), s32[]{:S(2)}) async-start(), calls=%async_computation.3 | async-start | bytes 2621440 | tf_op jit(solution)/shard_map/all_gather | solution.py:48
  15.3 33.7 %copy-start.1 = (bf16[32,16,2048]{2,1,0:T(8,128)(2,1)S(1)}, bf16[32,16,2048]{2,1,0:T(8,128)(2,1)}, u32[]{:S(2)}) copy-start(bf16[32,16,2048]{2,1,0:T(8,128)(2,1)} %param.4) | copy-start | bytes 6291460
  52.4 18.4 %all-to-all-start.1 = ((bf16[64,2,512]{2,1,0:T(2,128)(2,1)}), bf16[64,2,512]{2,1,0:T(2,128)(2,1)S(1)}, u32[]{:S(2)}, u32[]{:S(2)}) async-start(bf16[64,2,512]{2,1,0:T(2,128)(2,1)} %reshape.223), calls=%async_computation.1 | async-start | bytes 262144 | tf_op jit(solution)/shard_map/all_to_all | solution.py:42
Sparse Core Ops, SparseCore 0:
  49.1 29.8 all-gather.1
where the time goes:
time: 116 us; the launch traced here: 115 us
  blocking collectives  56 us (48%)
  waiting for transfers between devices  18.3 us (16%)
  between operations  13.5 us (12%)
  matrix products  11.6 us (10%)
  starting transfers between devices  6.93 us (6%)
  local copies, waits for them, and re-layouts  5.02 us (4%)
  other arithmetic  3.83 us (3%)
    all_to_all x1, blocking collectives, per_device(): lax.all_to_all(source_spec, 'af', split_axis=0, concat_axis=2, tiled=True)  32.5 us
    all_to_all x1, blocking collectives, per_device(): lax.all_to_all(predicted, 'af', split_axis=3, concat_axis=1, tiled=True)  23.5 us
    all_to_all x1, waiting for transfers between devices, per_device(): lax.all_to_all(receiver_spec, 'af', split_axis=0, concat_axis=2, tiled=True)  10.8 us
    all_gather x1, waiting for transfers between devices, per_device(): lax.all_gather(source_freq, 'row', axis=3, tiled=True)  7.53 us
    all_to_all x1, starting transfers between devices, per_device(): lax.all_to_all(receiver_spec, 'af', split_axis=0, concat_axis=2, tiled=True)  6.92 us
    dot_general x1, matrix products, per_device(): jnp.einsum('fct,skt->fcsk', forward, source_traces, preferred_element_typ...  6.26 us
    another operation x2, other arithmetic  3.78 us
    dot_general x1, matrix products, per_device(): jnp.einsum('fockr,fcsk->rfos', coupling(receiver_freq), lax.all_gather(so...  2.35 us
  transfers between devices with their start and end apart: 2, of which 2 were waited for; matrix products, arithmetic and copies ran while one was open for 4% of the time, Pallas kernels for 0%

commit v1 on v0

v1 whole, which is shorter than its diff:
```python
import math

import jax
import jax.numpy as jnp
import numpy as np
from jax import lax
from jax.sharding import Mesh, PartitionSpec as P

NT = 2048
NF = 64
F_LOW = 96
K = 1024

AXES = ("yh", "z1", "z0", "x", "yl", "core")
AF = ("yh", "z1", "z0", "x")
ROW = ("yl", "core")
GROUP = ("yh", "z0", "x", "yl", "core")


def tables(amplitude):
    samples = np.arange(NT, dtype=np.int64)
    frequency = F_LOW + np.arange(NF, dtype=np.int64)
    phase_index = frequency[:, None] * samples[None, :] % NT
    angles = phase_index.astype(np.float64) * (2.0 * math.pi / NT)
    return np.stack([np.cos(angles), -np.sin(angles)], axis=1) * amplitude


def per_device(source_traces, receiver_traces, wavelet_inverse):
    forward = jnp.asarray(tables(1.0 / math.sqrt(NT)), jnp.bfloat16)
    receiver_spec = jnp.einsum(
        "fct,rkt->fckr", forward, receiver_traces, preferred_element_type=jnp.float32
    ).astype(jnp.bfloat16)
    receiver_spec = receiver_spec.reshape(NF, -1)
    other = [
        lax.ppermute(receiver_spec, "z1", [(i, (i + hop) % 4) for i in range(4)])
        for hop in (2, 1, 3)
    ]
    source_spec = (
        jnp.einsum("fct,skt->fcsk", forward, source_traces, preferred_element_type=jnp.float32)
        .astype(jnp.bfloat16)
        .reshape(NF, -1)
    )
    sent = jnp.concatenate([source_spec, receiver_spec] + other, axis=1)
    got = lax.all_to_all(sent, GROUP, split_axis=0, concat_axis=0, tiled=True)
    n_src = 2 * 8 * 256
    source_freq = got[:, :n_src].reshape(2, 2, 4, 4, 2, 8, 256)
    source_freq = source_freq.transpose(4, 0, 1, 2, 5, 3, 6).reshape(2, 128, K)
    receiver_freq = got[:, n_src:].reshape(2, 2, 4, 4, 4, 2, 16, 32)
    own = lax.axis_index("z1")
    slots = jnp.array([0, 2, 1, 3], jnp.int32)
    order = slots[(own - jnp.arange(4)) % 4]
    receiver_freq = receiver_freq.transpose(4, 5, 0, 1, 2, 6, 3, 7)
    receiver_freq = jnp.take(receiver_freq, order, axis=0)
    receiver_freq = receiver_freq.transpose(1, 2, 0, 3, 4, 5, 6, 7).reshape(2, K, 128)
    real, imag = receiver_freq[0], receiver_freq[1]
    coupled = jnp.concatenate(
        [jnp.concatenate([real, imag], axis=1), jnp.concatenate([-imag, real], axis=1)], axis=0
    )
    raw = jnp.einsum(
        "sk,kr->sr",
        jnp.concatenate([source_freq[0], source_freq[1]], axis=1),
        coupled,
        preferred_element_type=jnp.float32,
    )
    raw_real, raw_imag = raw[:, :128], raw[:, 128:]
    wavelet = lax.dynamic_slice_in_dim(wavelet_inverse, lax.axis_index(GROUP), 1, 0)
    wave_real, wave_imag = wavelet[0, 0], wavelet[0, 1]
    amplitude = 1.0 / math.sqrt(K)
    pred_real = (raw_real * wave_real - raw_imag * wave_imag) * amplitude
    pred_imag = (raw_real * wave_imag + raw_imag * wave_real) * amplitude
    predicted = jnp.stack([pred_real, pred_imag]).astype(jnp.bfloat16)
    predicted = predicted.reshape(2, 16, 8, 4, 32).transpose(1, 3, 0, 2, 4).reshape(NF, 2, 256)
    returned = lax.all_to_all(predicted, GROUP, split_axis=0, concat_axis=0, tiled=True)
    inverse = jnp.asarray(tables(1.0 / math.sqrt(NF)), jnp.bfloat16)
    result = jnp.einsum("fcm,fct->mt", returned, inverse, preferred_element_type=jnp.float32)
    return result.astype(jnp.bfloat16).reshape(8, 32, NT)


def solution(mesh):
    fine = Mesh(np.asarray(mesh.devices).reshape(2, 4, 2, 4, 2, 2), AXES)
    return jax.shard_map(
        per_device,
        mesh=fine,
        in_specs=(P(AF, ROW, None), P(ROW, AF, None), P()),
        out_specs=P(AF, ROW, None),
        check_vma=False,
    )
```

time: 116 us -> 82.2 us (0.71)
  blocking collectives: 56 us -> 13.7 us
  between operations: 13.5 us -> 0.31 us
  starting transfers between devices: 6.93 us -> 19.4 us
  local copies, waits for them, and re-layouts: 5.02 us -> 15.2 us
    all_to_all x2 -> x1, blocking collectives: 56 us -> 13.7 us  [per_device(): lax.all_to_all(predicted, GROUP, split_axis=0, concat_axis=0, tiled=True)]
    ppermute x0 -> x3, starting transfers between devices: none -> 11.4 us  [per_device(): lax.ppermute(receiver_spec, 'z1', [(i, (i + hop) % 4) for i in range(4)])]
    all_gather x1 -> x0, waiting for transfers between devices: 7.53 us -> none  [per_device(): lax.all_gather(source_freq, 'row', axis=3, tiled=True)]
    all_to_all x1, waiting for transfers between devices: 10.8 us -> 15.7 us  [per_device(): got = lax.all_to_all(sent, GROUP, split_axis=0, concat_axis=0, tiled=True)]
    reshape x0 -> x4, local copies, waits for them, and re-layouts: none -> 3.9 us  [the longest x2 3.59 us: per_device(): receiver_freq = got[:, n_src:].reshape(2, 2, 4, 4, 4, 2, 16, 32)]
    gather x0 -> x2, local copies, waits for them, and re-layouts: none -> 3.18 us  [the longest x1 2.54 us: per_device(): receiver_freq = jnp.take(receiver_freq, order, axis=0)]
    ppermute x0 -> x3, waiting for transfers between devices: none -> 2.93 us  [per_device(): lax.ppermute(receiver_spec, 'z1', [(i, (i + hop) % 4) for i in range(4)])]
    another operation x4 -> x1, other arithmetic: 3.81 us -> 1.3 us
  transfers between devices with their start and end apart: 2 -> 4, of which waited for: 2 -> 2; matrix products, arithmetic and copies ran while one was open for 4% -> 9% of each run, Pallas kernels for 0% -> 0%
where the time goes in v1:
time: 82.2 us; the launch traced here: 81.9 us
  starting transfers between devices  19.4 us (24%)
  waiting for transfers between devices  18.6 us (23%)
  local copies, waits for them, and re-layouts  15.2 us (18%)
  blocking collectives  13.7 us (17%)
  matrix products  11.3 us (14%)
  other arithmetic  3.32 us (4%)
    all_to_all x1, waiting for transfers between devices, per_device(): got = lax.all_to_all(sent, GROUP, split_axis=0, concat_axis=0, tiled=True)  15.7 us
    all_to_all x1, blocking collectives, per_device(): lax.all_to_all(predicted, GROUP, split_axis=0, concat_axis=0, tiled=True)  13.7 us
    ppermute x3, starting transfers between devices, per_device(): lax.ppermute(receiver_spec, 'z1', [(i, (i + hop) % 4) for i in range(4)])  11.4 us
    all_to_all x1, starting transfers between devices, per_device(): got = lax.all_to_all(sent, GROUP, split_axis=0, concat_axis=0, tiled=True)  8.04 us
    dot_general x1, matrix products, per_device(): jnp.einsum('fct,skt->fcsk', forward, source_traces, preferred_element_typ...  6.26 us
    unnamed x17, local copies, waits for them, and re-layouts  4 us
    reshape x2, local copies, waits for them, and re-layouts, per_device(): receiver_freq = got[:, n_src:].reshape(2, 2, 4, 4, 4, 2, 16, 32)  3.59 us
    dot_general x1, matrix products, per_device(): jnp.einsum('fct,rkt->fckr', forward, receiver_traces, preferred_element_t...  3.34 us
  transfers between devices with their start and end apart: 4, of which 2 were waited for; matrix products, arithmetic and copies ran while one was open for 9% of the time, Pallas kernels for 0%

profile of v1, /device:TPU:1, one launch (start us, length us, event | category | flops | bytes accessed | tf_op | source)
XLA Modules:
  0.0 81.9 jit_solution(14726836172117363167)
XLA Ops:
  0.0 3.3 %fusion.9 = bf16[64,2,32,16]{0,2,3,1:T(8,128)(2,1)S(1)} fusion(bf16[64,2,2048,1]{2,0,3,1:T(8,128)(2,1)} %constant.75, bf16[32,16,2048]{2,1,0:T(8,128)(2,1)} %param.7), kind=kOutput, calls=%fused_computation.12 | convolution fusion | flops 268500992 | bytes 2752512 | tf_op jit(solution)/shard_map/fct,rkt->fckr/dot_general | solution.py:30
  3.5 7.8 %collective-permute-start = (bf16[64,1024]{1,0:T(8,128)(2,1)S(1)}, bf16[64,1024]{1,0:T(8,128)(2,1)S(1)}, u32[]{:S(2)}, u32[]{:S(2)}) collective-permute-start(bf16[64,1024]{1,0:T(8,128)(2,1)S(1)} %copy.56), channel_id=1, source_target_pairs={{0,64},{32,96},{64,0},{96,32},{1,65},{33,97},{65,1},{97,33},{2,66}... | collective-permute-start | bytes 393224 | tf_op jit(solution)/shard_map/ppermute | solution.py:35
  11.3 1.2 %collective-permute-start.1 = (bf16[64,1024]{1,0:T(8,128)(2,1)S(1)}, bf16[64,1024]{1,0:T(8,128)(2,1)S(1)}, u32[]{:S(2)}, u32[]{:S(2)}) collective-permute-start(bf16[64,1024]{1,0:T(8,128)(2,1)S(1)} %copy.56), channel_id=1, source_target_pairs={{0,32},{32,64},{64,96},{96,0},{1,33},{33,65},{65,97},{97,1},{2,34}... | collective-permute-start | bytes 393224 | tf_op jit(solution)/shard_map/ppermute | solution.py:35
  12.5 2.4 %collective-permute-start.2 = (bf16[64,1024]{1,0:T(8,128)(2,1)S(1)}, bf16[64,1024]{1,0:T(8,128)(2,1)S(1)}, u32[]{:S(2)}, u32[]{:S(2)}) collective-permute-start(bf16[64,1024]{1,0:T(8,128)(2,1)S(1)} %copy.56), channel_id=1, source_target_pairs={{0,96},{32,0},{64,32},{96,64},{1,97},{33,1},{65,33},{97,65},{2,98}... | collective-permute-start | bytes 393224 | tf_op jit(solution)/shard_map/ppermute | solution.py:35
  14.9 6.3 %fusion.6 = bf16[64,2,8,256]{3,0,2,1:T(8,128)(2,1)S(1)} fusion(bf16[64,2,2048,1]{2,0,3,1:T(8,128)(2,1)S(1)} %copy-done.3, bf16[8,256,2048]{2,1,0:T(8,128)(2,1)} %param.6), kind=kOutput, calls=%fused_computation.11 | convolution fusion | flops 1074003968 | bytes 9437184 | tf_op jit(solution)/shard_map/fct,skt->fcsk/dot_general | solution.py:39
  21.3 2.9 %collective-permute-done.2 = bf16[64,1024]{1,0:T(8,128)(2,1)S(1)} collective-permute-done((bf16[64,1024]{1,0:T(8,128)(2,1)S(1)}, bf16[64,1024]{1,0:T(8,128)(2,1)S(1)}, u32[]{:S(2)}, u32[]{:S(2)}) %collective-permute-start.2) | collective-permute-done | bytes 131104 | tf_op jit(solution)/shard_map/ppermute | solution.py:35
  24.3 0.5 broadcast.121
  24.8 1.4 %reduce = bf16[64,8192]{1,0:T(8,128)(2,1)S(1)} reduce(bf16[64,1,8192]{2,0,1:T(8,128)(2,1)S(1)} %bitcast.58, bf16[]{:T(256)} %broadcast.121), dimensions={1}, to_apply=%copy.57.reduce_sub_computation | reduce | bytes 2097154 | tf_op jit(solution)/shard_map/all_to_all | solution.py:44
  26.2 1.6 %reshape.130 = bf16[64,2,4096]{2,1,0:T(2,128)(2,1)} reshape(bf16[64,8192]{1,0:T(8,128)(2,1)S(1)} %reduce) | data formatting | bytes 2097152
  27.8 8.0 %all-to-all-start = ((bf16[64,2,4096]{2,1,0:T(2,128)(2,1)}), bf16[64,2,4096]{2,1,0:T(2,128)(2,1)S(1)}, u32[]{:S(2)}, u32[]{:S(2)}) async-start(bf16[64,2,4096]{2,1,0:T(2,128)(2,1)} %reshape.130), calls=%async_computation | async-start | bytes 2097152 | tf_op jit(solution)/shard_map/all_to_all | solution.py:44
  35.9 0.6 gather_fusion
  36.6 0.6 fusion.31
  37.2 15.7 %all-to-all-done = bf16[64,2,4096]{2,1,0:T(2,128)(2,1)S(1)} async-done(((bf16[64,2,4096]{2,1,0:T(2,128)(2,1)}), bf16[64,2,4096]{2,1,0:T(2,128)(2,1)S(1)}, u32[]{:S(2)}, u32[]{:S(2)}) %all-to-all-start) | async-done | bytes 1048608 | tf_op jit(solution)/shard_map/all_to_all | solution.py:44
  52.9 1.0 %reshape.131 = bf16[64,1,8192]{2,1,0:T(2,128)(2,1)S(1)} reshape(bf16[64,2,4096]{2,1,0:T(2,128)(2,1)S(1)} %all-to-all-done) | data formatting | bytes 2097152
  54.0 1.1 %copy.79 = bf16[64,1,8192]{2,0,1:T(8,128)(2,1)S(1)} copy(bf16[64,1,8192]{2,1,0:T(2,128)(2,1)S(1)} %reshape.131) | data formatting | bytes 2097152
  55.2 1.6 %reshape.107 = bf16[2,2,4,4,4,2,16,32]{7,6,5,4,3,2,1,0:T(8,128)(2,1)S(1)} reshape(bf16[64,4096]{1,0:T(8,128)(2,1)S(1)} %get-tuple-element.8) | data formatting | bytes 1048576 | tf_op jit(solution)/shard_map/reshape | solution.py:48
  56.8 1.9 %copy.78 = bf16[2,2,4,4,4,2,16,32]{7,6,3,2,1,0,5,4:T(8,128)(2,1)} copy(bf16[2,2,4,4,4,2,16,32]{7,6,5,4,3,2,1,0:T(8,128)(2,1)S(1)} %reshape.107) | data formatting | bytes 1048576 | tf_op jit(solution)/shard_map/reshape | solution.py:48
  58.8 2.5 %gather_fusion.1 = bf16[4,2,2,2,4,16,4,32]{7,5,6,4,3,2,1,0:T(8,128)(2,1)S(1)} fusion(bf16[4,2,2,2,4,16,4,32]{7,5,6,4,3,2,1,0:T(8,128)(2,1)} %bitcast.56, s32[1024]{0:T(1024)S(1)} %pad_clamp_fusion), kind=kCustom, calls=%fused_computation.1 | custom fusion | bytes 1048592 | tf_op jit(solution)/shard_map/jit(_take)/gather | solution.py:53
  62.1 0.5 copy.60
  62.6 0.5 squeeze.21
  63.2 0.5 copy.59
  64.8 1.3 %multiply_convert_fusion.1 = (bf16[128,128]{1,0:T(8,128)(2,1)S(1)}, bf16[128,128]{1,0:T(8,128)(2,1)S(1)}) fusion(f32[128,256]{1,0:T(8,128)S(1)} %fusion.12, f32[]{:T(128)} %bitcast.18, f32[]{:T(128)} %bitcast.17), kind=kLoop, calls=%fused_computation.28 | loop fusion | flops 163840 | bytes 196616 | tf_op jit(solution)/shard_map/convert.3
  66.8 13.7 %all_to_all.17 = bf16[64,2,256]{2,1,0:T(2,128)(2,1)S(1)} all-to-all(bf16[64,2,256]{2,1,0:T(2,128)(2,1)S(1)} %reshape.108), channel_id=1, replica_groups=mesh['yh'=2,'z1'=4,'z0'=2,'x'=4,'yl'=2,'core'=2] {'yh','z0','x','yl','co..., dimensions={0} | all-to-all | bytes 131072 | tf_op jit(solution)/shard_map/all_to_all | solution.py:73
  80.5 1.4 %fusion.2 = bf16[256,2048]{1,0:T(8,128)(2,1)} fusion(bf16[64,2,2048]{2,0,1:T(8,128)(2,1)S(1)} %copy-done.2, bf16[64,2,256]{2,1,0:T(2,128)(2,1)S(1)} %all_to_all.17), kind=kOutput, calls=%fused_computation.5 | convolution fusion | flops 134742016 | bytes 1638400 | tf_op jit(solution)/shard_map/fcm,fct->mt/dot_general | solution.py:75
  (36 shorter events, 2.9 us)
Async XLA Ops:
  0.0 36.6 %copy-start = (f32[64,2]{0,1:T(2,128)S(1)}, f32[64,2]{0,1:T(2,128)}, u32[]{:S(2)}) copy-start(f32[64,2]{0,1:T(2,128)} %param.8) | copy-start | bytes 1540
  0.0 14.9 %copy-start.3 = (bf16[64,2,2048,1]{2,0,3,1:T(8,128)(2,1)S(1)}, bf16[64,2,2048,1]{2,0,3,1:T(8,128)(2,1)}, u32[]{:S(2)}) copy-start(bf16[64,2,2048,1]{2,0,3,1:T(8,128)(2,1)} %constant.75) | copy-start | bytes 1572868
  3.5 17.8 %collective-permute-start = (bf16[64,1024]{1,0:T(8,128)(2,1)S(1)}, bf16[64,1024]{1,0:T(8,128)(2,1)S(1)}, u32[]{:S(2)}, u32[]{:S(2)}) collective-permute-start(bf16[64,1024]{1,0:T(8,128)(2,1)S(1)} %copy.56), channel_id=1, source_target_pairs={{0,64},{32,96},{64,0},{96,32},{1,65},{33,97},{65,1},{97,33},{2,66}... | collective-permute-start | bytes 393224 | tf_op jit(solution)/shard_map/ppermute | solution.py:35
  11.3 10.0 %collective-permute-start.1 = (bf16[64,1024]{1,0:T(8,128)(2,1)S(1)}, bf16[64,1024]{1,0:T(8,128)(2,1)S(1)}, u32[]{:S(2)}, u32[]{:S(2)}) collective-permute-start(bf16[64,1024]{1,0:T(8,128)(2,1)S(1)} %copy.56), channel_id=1, source_target_pairs={{0,32},{32,64},{64,96},{96,0},{1,33},{33,65},{65,97},{97,1},{2,34}... | collective-permute-start | bytes 393224 | tf_op jit(solution)/shard_map/ppermute | solution.py:35
  12.5 11.7 %collective-permute-start.2 = (bf16[64,1024]{1,0:T(8,128)(2,1)S(1)}, bf16[64,1024]{1,0:T(8,128)(2,1)S(1)}, u32[]{:S(2)}, u32[]{:S(2)}) collective-permute-start(bf16[64,1024]{1,0:T(8,128)(2,1)S(1)} %copy.56), channel_id=1, source_target_pairs={{0,96},{32,0},{64,32},{96,64},{1,97},{33,1},{65,33},{97,65},{2,98}... | collective-permute-start | bytes 393224 | tf_op jit(solution)/shard_map/ppermute | solution.py:35
  26.2 9.7 %copy-start.1 = (s32[4]{0:T(128)S(1)}, s32[4]{0:T(128)}, u32[]{:S(2)}) copy-start(s32[4]{0:T(128)} %constant.71.clone) | copy-start | bytes 52
  27.8 25.1 %all-to-all-start = ((bf16[64,2,4096]{2,1,0:T(2,128)(2,1)}), bf16[64,2,4096]{2,1,0:T(2,128)(2,1)S(1)}, u32[]{:S(2)}, u32[]{:S(2)}) async-start(bf16[64,2,4096]{2,1,0:T(2,128)(2,1)} %reshape.130), calls=%async_computation | async-start | bytes 2097152 | tf_op jit(solution)/shard_map/all_to_all | solution.py:44
  64.8 15.7 %copy-start.2 = (bf16[64,2,2048]{2,0,1:T(8,128)(2,1)S(1)}, bf16[64,2,2048]{2,0,1:T(8,128)(2,1)}, u32[]{:S(2)}) copy-start(bf16[64,2,2048]{2,0,1:T(8,128)(2,1)} %constant.72.clone) | copy-start | bytes 1572868

commit v2 on v1

v2 whole, which is shorter than its diff:
```python
import math

import jax
import jax.numpy as jnp
import numpy as np
from jax import lax
from jax.experimental import pallas as pl
from jax.experimental.pallas import tpu as pltpu
from jax.sharding import Mesh, PartitionSpec as P

NT = 2048
NF = 64
F_LOW = 96
K = 1024

AXES = ("yh", "z1", "z0", "x", "yl", "core")
AF = ("yh", "z1", "z0", "x")
ROW = ("yl", "core")
GROUP = ("yh", "z0", "x", "yl", "core")
HOPS = (2, 1, 3)
SLOTS = (0,) + HOPS

VMEM = pl.BlockSpec(memory_space=pltpu.VMEM)
SMEM = pl.BlockSpec(memory_space=pltpu.SMEM)
HBM = pl.BlockSpec(memory_space=pl.ANY)


def tables(amplitude):
    samples = np.arange(NT, dtype=np.int64)
    frequency = F_LOW + np.arange(NF, dtype=np.int64)
    phase_index = frequency[:, None] * samples[None, :] % NT
    angles = phase_index.astype(np.float64) * (2.0 * math.pi / NT)
    both = np.stack([np.cos(angles), -np.sin(angles)], axis=1) * amplitude
    return both.astype(jnp.bfloat16)


def mover(sizes, order):
    n = math.prod(sizes)
    source = np.arange(n).reshape(sizes).transpose(order).reshape(-1)
    matrix = np.zeros((n, n), np.float32)
    matrix[source, np.arange(n)] = 1.0
    return matrix.astype(jnp.bfloat16)


def dot(a, b, dims=((1,), (0,))):
    return lax.dot_general(a, b, (dims, ((), ())), preferred_element_type=jnp.float32)


def receiver_kernel(x_hbm, table_hbm, mover_hbm, out_ref, x, table, moves, arrived, rows):
    copies = [
        pltpu.make_async_copy(table_hbm, table, arrived.at[0]),
        pltpu.make_async_copy(x_hbm, x, arrived.at[1]),
        pltpu.make_async_copy(mover_hbm, moves, arrived.at[2]),
    ]
    for copy in copies:
        copy.start()
    copies[0].wait()
    copies[1].wait()
    spectra = dot(x[...].reshape(512, NT), table[...]).astype(jnp.bfloat16)
    copies[2].wait()
    moved = dot(spectra, moves[...], ((0,), (0,)))
    low = lax.broadcasted_iota(jnp.int32, (NF, 128), 1) < 64
    for pair in range(4):
        real = moved[:NF, pair * 128 : (pair + 1) * 128]
        imag = moved[NF:, pair * 128 : (pair + 1) * 128]
        even = jnp.where(low, real, pltpu.roll(imag, 64, 1))
        odd = jnp.where(low, pltpu.roll(real, 64, 1), imag)
        rows[pl.ds(2 * pair, NF, stride=8), :] = even
        rows[pl.ds(2 * pair + 1, NF, stride=8), :] = odd
    out_ref[...] = rows[...].astype(jnp.bfloat16)


def receiver_spectra(traces, table):
    return pl.pallas_call(
        receiver_kernel,
        out_shape=jax.ShapeDtypeStruct((NF * 8, 128), jnp.bfloat16),
        in_specs=[HBM] * 3,
        out_specs=VMEM,
        scratch_shapes=[
            pltpu.VMEM((32, 16, NT), jnp.bfloat16),
            pltpu.VMEM((NT, 128), jnp.bfloat16),
            pltpu.VMEM((512, 512), jnp.bfloat16),
            pltpu.SemaphoreType.DMA((3,)),
            pltpu.VMEM((NF * 8, 128), jnp.float32),
        ],
        compiler_params=pltpu.CompilerParams(vmem_limit_bytes=60 << 20),
        cost_estimate=pl.CostEstimate(
            flops=2 * 512 * 128 * NT, bytes_accessed=3 << 20, transcendentals=0
        ),
        name="receiver_spectra",
    )(traces, table, jnp.asarray(mover((32, 8, 2), (1, 2, 0))))


AT_ONCE = 2


def source_kernel(x_hbm, own_hbm, table_hbm, out_ref, x, own, table, arrived, ready, rows):
    others = [
        pltpu.make_async_copy(table_hbm, table, ready.at[0]),
        pltpu.make_async_copy(own_hbm, own, ready.at[1]),
    ]
    others[0].start()
    for s in range(8):
        pltpu.make_async_copy(x_hbm.at[s], x.at[s], arrived.at[s]).start()
    others[1].start()
    others[0].wait()

    @pl.loop(0, 8 // AT_ONCE)
    def _(step):
        first = step * AT_ONCE
        for j in range(AT_ONCE):
            s = first + j
            pltpu.make_async_copy(x_hbm.at[s], x.at[s], arrived.at[s]).wait()
        traces = x[pl.ds(first, AT_ONCE)].reshape(AT_ONCE * 256, NT)
        spectra = dot(traces, table[...]).T
        for j in range(AT_ONCE):
            for c in range(2):
                for kh in range(2):
                    at = j * 256 + kh * 128
                    rows[pl.ds(kh * 16 + c * 8 + first + j, NF, stride=32), :] = spectra[
                        c * NF : (c + 1) * NF, at : at + 128
                    ]

    others[1].wait()
    out_ref[:, :32, :] = rows[...].astype(jnp.bfloat16).reshape(NF, 32, 128)
    out_ref[:, 32:40, :] = own[...].reshape(NF, 8, 128)


def source_spectra(traces, own, table):
    return pl.pallas_call(
        source_kernel,
        out_shape=jax.ShapeDtypeStruct((NF, 64, 128), jnp.bfloat16),
        in_specs=[HBM] * 3,
        out_specs=VMEM,
        scratch_shapes=[
            pltpu.VMEM((8, 256, NT), jnp.bfloat16),
            pltpu.VMEM((NF * 8, 128), jnp.bfloat16),
            pltpu.VMEM((NT, 128), jnp.bfloat16),
            pltpu.SemaphoreType.DMA((8,)),
            pltpu.SemaphoreType.DMA((2,)),
            pltpu.VMEM((NF * 32, 128), jnp.float32),
        ],
        compiler_params=pltpu.CompilerParams(vmem_limit_bytes=60 << 20),
        cost_estimate=pl.CostEstimate(
            flops=2 * 2048 * 128 * NT, bytes_accessed=10 << 20, transcendentals=0
        ),
        name="source_spectra",
    )(traces, own, table)


def product_kernel(z1_ref, wave_ref, got_ref, mover_ref, back_ref, out_ref, right, pred, rows):
    z1 = z1_ref[0]
    raw = jnp.zeros((256, 256), jnp.float32)
    for pair in range(2):
        at = 32 + 16 * pair
        pieces = [got_ref[:, row, at : at + 16, :].reshape(256, 128) for row in range(4)]
        moved = dot(jnp.concatenate(pieces, axis=1), mover_ref[...]).reshape(2, 8, 2, 8, 512)
        for half in range(2):
            slot = 2 * pair + half
            origin = lax.rem(z1 - SLOTS[slot] + 4, 4)
            left = []
            for yh in range(2):
                panel = 2 * yh + lax.div(origin, 2)
                start = pl.multiple_of(16 * lax.rem(origin, 2), 16)
                left.append(got_ref[:, panel, pl.ds(start, 16), :].reshape(256, 128))
                part = moved[yh, :, half].reshape(64, 512)
                for k in range(2):
                    for c in range(2):
                        at = 256 * k + 128 * c
                        right[slot, c, pl.ds(yh * 128 + k, 64, stride=2), :] = part[:, at : at + 128]
            coupled = jnp.concatenate([right[slot, 0], right[slot, 1]], axis=1)
            raw += dot(
                jnp.concatenate(left, axis=1),
                coupled.astype(jnp.bfloat16),
            )
    raw = raw.reshape(16, 2, 8, 256)
    real = raw[:, 0, :, :128] - raw[:, 1, :, 128:]
    imag = raw[:, 0, :, 128:] + raw[:, 1, :, :128]
    amplitude = 1.0 / math.sqrt(K)
    wave_real, wave_imag = wave_ref[0], wave_ref[1]
    pred[0] = ((real * wave_real - imag * wave_imag) * amplitude).reshape(128, 128)
    pred[1] = ((real * wave_imag + imag * wave_real) * amplitude).reshape(128, 128)
    wide = []
    for c in range(2):
        for high in range(2):
            wide.append(
                jnp.concatenate(
                    [pred[c, pl.ds(high * 4 + low, 16, stride=8), :] for low in range(4)], axis=1
                )
            )
    wide = dot(jnp.concatenate(wide, axis=0).astype(jnp.bfloat16), back_ref[...])
    for q in range(4):
        for row in range(4):
            rows[pl.ds(row * 4 + q, 16, stride=16), :] = wide[
                q * 16 : (q + 1) * 16, row * 128 : (row + 1) * 128
            ]
    out_ref[...] = rows[...].astype(jnp.bfloat16)


def predicted_spectra(got, z1, wavelet):
    return pl.pallas_call(
        product_kernel,
        out_shape=jax.ShapeDtypeStruct((256, 128), jnp.bfloat16),
        in_specs=[SMEM, SMEM] + [VMEM] * 3,
        out_specs=VMEM,
        scratch_shapes=[
            pltpu.VMEM((4, 2, 256, 128), jnp.float32),
            pltpu.VMEM((2, 128, 128), jnp.float32),
            pltpu.VMEM((256, 128), jnp.float32),
        ],
        compiler_params=pltpu.CompilerParams(vmem_limit_bytes=16 << 20),
        cost_estimate=pl.CostEstimate(flops=4 << 28, bytes_accessed=2 << 20, transcendentals=0),
        name="predicted_spectra",
    )(
        z1,
        wavelet,
        got.reshape(16, 4, 64, 128),
        jnp.asarray(mover((4, 2, 2, 32), (2, 1, 0, 3))),
        jnp.asarray(mover((4, 4, 32), (1, 0, 2))),
    )


def multiples_kernel(x_ref, table_ref, out_ref, rows):
    rows[...] = x_ref[...].astype(jnp.float32)
    half = rows[pl.ds(pl.program_id(0), 128, stride=2), :].astype(jnp.bfloat16)
    out_ref[...] = dot(half, table_ref[...], ((0,), (0,))).astype(jnp.bfloat16)


def multiples(returned):
    table = jnp.asarray(tables(1.0 / math.sqrt(NF)).reshape(2 * NF, NT))
    return pl.pallas_call(
        multiples_kernel,
        grid=(2,),
        out_shape=jax.ShapeDtypeStruct((256, NT), jnp.bfloat16),
        in_specs=[
            pl.BlockSpec((256, 128), lambda i: (0, 0)),
            pl.BlockSpec((128, NT), lambda i: (0, 0)),
        ],
        out_specs=pl.BlockSpec((128, NT), lambda i: (i, 0)),
        scratch_shapes=[pltpu.VMEM((256, 128), jnp.float32)],
        compiler_params=pltpu.CompilerParams(vmem_limit_bytes=24 << 20),
        cost_estimate=pl.CostEstimate(
            flops=2 * 256 * 128 * NT, bytes_accessed=2 << 20, transcendentals=0
        ),
        name="multiples",
    )(returned, table)


def per_device(source_traces, receiver_traces, wavelet_inverse):
    table = jnp.asarray(tables(1.0 / math.sqrt(NT)).transpose(2, 1, 0).reshape(NT, 2 * NF))
    own = receiver_spectra(receiver_traces, table)
    others = [lax.ppermute(own, "z1", [(i, (i + hop) % 4) for i in range(4)]) for hop in HOPS]
    sent = source_spectra(source_traces, own, table)
    others = jnp.concatenate([other.reshape(NF, 8, 128) for other in others], axis=1)
    sent = lax.dynamic_update_slice(sent, others, (0, 40, 0))
    got = lax.all_to_all(sent, GROUP, split_axis=0, concat_axis=0, tiled=True)
    wavelet = lax.dynamic_slice_in_dim(wavelet_inverse, lax.axis_index(GROUP), 1, 0).reshape(2)
    predicted = predicted_spectra(got, lax.axis_index("z1").reshape(1), wavelet)
    returned = lax.all_to_all(
        predicted.reshape(NF, 4, 128), GROUP, split_axis=0, concat_axis=0, tiled=True
    )
    return multiples(returned.reshape(256, 128)).reshape(8, 32, NT)


def solution(mesh):
    fine = Mesh(np.asarray(mesh.devices).reshape(2, 4, 2, 4, 2, 2), AXES)
    return jax.shard_map(
        per_device,
        mesh=fine,
        in_specs=(P(AF, ROW, None), P(ROW, AF, None), P()),
        out_specs=P(AF, ROW, None),
        check_vma=False,
    )
```

time: 82.2 us -> 70.4 us (0.86)
  local copies, waits for them, and re-layouts: 15.2 us -> 0.2 us
  Pallas kernels: 0 us -> 14.8 us
  matrix products: 11.3 us -> 0 us
  starting transfers between devices: 19.4 us -> 23.6 us
  other arithmetic: 3.32 us -> 0.81 us
  waiting for transfers between devices: 18.6 us -> 17 us
    pallas_call x0 -> x4, Pallas kernels: none -> 14.8 us  [the longest x1 7.74 us: source_spectra(): pl.pallas_call(source_kernel, out_shape=jax.ShapeDtypeStruct((NF, 64, 128...]
    dot_general x4 -> x0, matrix products: 11.3 us -> none  [the longest x1 6.26 us: per_device(): jnp.einsum('fct,skt->fcsk', forward, source_traces, preferred_element_typ...]
    all_to_all x1, starting transfers between devices: 8.04 us -> 13.4 us  [per_device(): got = lax.all_to_all(sent, GROUP, split_axis=0, concat_axis=0, tiled=True)]
    unnamed x17 -> x8, local copies, waits for them, and re-layouts: 4 us -> 0.02 us
    reshape x4 -> x0, local copies, waits for them, and re-layouts: 3.9 us -> none  [the longest x2 3.59 us: per_device(): receiver_freq = got[:, n_src:].reshape(2, 2, 4, 4, 4, 2, 16, 32)]
    gather x2 -> x0, local copies, waits for them, and re-layouts: 3.18 us -> none  [the longest x1 2.54 us: per_device(): receiver_freq = jnp.take(receiver_freq, order, axis=0)]
    ppermute x3, waiting for transfers between devices: 2.93 us -> 0.18 us  [per_device(): lax.ppermute(own, 'z1', [(i, (i + hop) % 4) for i in range(4)])]
    slice x6 -> x0, local copies, waits for them, and re-layouts: 2.26 us -> none  [the longest x3 1.54 us: per_device(): real, imag = (receiver_freq[0], receiver_freq[1])]
  transfers between devices with their start and end apart: 4 -> 4, of which waited for: 2 -> 2; matrix products, arithmetic and copies ran while one was open for 9% -> 0% of each run, Pallas kernels for 0% -> 11%
where the time goes in v2:
time: 70.4 us; the launch traced here: 70.2 us
  starting transfers between devices  23.6 us (34%)
  waiting for transfers between devices  17 us (24%)
  Pallas kernels  14.8 us (21%)
  blocking collectives  13.7 us (19%)
  other arithmetic  0.81 us (1%)
    all_to_all x1, waiting for transfers between devices, per_device(): got = lax.all_to_all(sent, GROUP, split_axis=0, concat_axis=0, tiled=True)  16.8 us
    all_to_all x1, blocking collectives, per_device(): lax.all_to_all(predicted.reshape(NF, 4, 128), GROUP, split_axis=0, concat...  13.7 us
    all_to_all x1, starting transfers between devices, per_device(): got = lax.all_to_all(sent, GROUP, split_axis=0, concat_axis=0, tiled=True)  13.4 us
    ppermute x3, starting transfers between devices, per_device(): lax.ppermute(own, 'z1', [(i, (i + hop) % 4) for i in range(4)])  10.2 us
    pallas_call x1, Pallas kernels, source_spectra(): pl.pallas_call(source_kernel, out_shape=jax.ShapeDtypeStruct((NF, 64, 128...  7.74 us
    pallas_call x1, Pallas kernels, receiver_spectra(): pl.pallas_call(receiver_kernel, out_shape=jax.ShapeDtypeStruct((NF * 8, 1...  3.69 us
    pallas_call x1, Pallas kernels, predicted_spectra(): pl.pallas_call(product_kernel, out_shape=jax.ShapeDtypeStruct((256, 128),...  1.9 us
    pallas_call x1, Pallas kernels, multiples(): pl.pallas_call(multiples_kernel, grid=(2,), out_shape=jax.ShapeDtypeStruc...  1.47 us
  transfers between devices with their start and end apart: 4, of which 2 were waited for; matrix products, arithmetic and copies ran while one was open for 0% of the time, Pallas kernels for 11%

profile of v2, /device:TPU:1, one launch (start us, length us, event | category | flops | bytes accessed | tf_op | source)
XLA Modules:
  0.0 70.2 jit_solution(10162873223327096347)
XLA Ops:
  0.0 0.0 copy-start
  0.0 0.0 copy-start.2
  0.0 0.0 copy-start.3
  0.0 3.7 %receiver_spectra.1.own_hbm = bf16[512,128]{1,0:T(8,128)(2,1)} custom-call(bf16[32,16,2048]{2,1,0:T(8,128)(2,1)} %x_hbm.2, bf16[2048,128]{1,0:T(8,128)(2,1)} %constant.47.clone.table_hbm, bf16[512,512]{1,0:T(8,128)(2,1)} %constant.48.clone.mover_hbm), custom_call_target="tpu_custom_call" | custom-call | flops 268435456 | bytes 3145728 | tf_op jit(solution)/shard_map/receiver_spectra/pallas_call | solution.py:74
  3.7 0.0 copy-start.1
  3.7 6.9 %collective-permute-start.2 = (bf16[512,128]{1,0:T(8,128)(2,1)}, bf16[512,128]{1,0:T(8,128)(2,1)S(1)}, u32[]{:S(2)}, u32[]{:S(2)}) collective-permute-start(bf16[512,128]{1,0:T(8,128)(2,1)} %receiver_spectra.1.own_hbm), channel_id=1, source_target_pairs={{0,96},{32,0},{64,32},{96,64},{1,97},{33,1},{65,33},{97,65},{2,98}... | collective-permute-start | bytes 393224 | tf_op jit(solution)/shard_map/ppermute | solution.py:252
  10.7 0.0 collective-permute-start.1
  10.7 3.3 %collective-permute-start = (bf16[512,128]{1,0:T(8,128)(2,1)}, bf16[512,128]{1,0:T(8,128)(2,1)S(1)}, u32[]{:S(2)}, u32[]{:S(2)}) collective-permute-start(bf16[512,128]{1,0:T(8,128)(2,1)} %receiver_spectra.1.own_hbm), channel_id=1, source_target_pairs={{0,64},{32,96},{64,0},{96,32},{1,65},{33,97},{65,1},{97,33},{2,66}... | collective-permute-start | bytes 393224 | tf_op jit(solution)/shard_map/ppermute | solution.py:252
  13.9 7.7 %source_spectra.1 = bf16[64,64,128]{2,1,0:T(8,128)(2,1)} custom-call(bf16[8,256,2048]{2,1,0:T(8,128)(2,1)} %x_hbm.3, bf16[512,128]{1,0:T(8,128)(2,1)} %receiver_spectra.1.own_hbm, bf16[2048,128]{1,0:T(8,128)(2,1)} %constant.47.clone.table_hbm), custom_call_target="tpu_custom_call" | custom-call | flops 1073741824 | bytes 10485760 | tf_op jit(solution)/shard_map/source_spectra/pallas_call | solution.py:130
  21.7 0.0 collective-permute-done.2
  21.7 0.0 collective-permute-done.1
  21.7 0.2 collective-permute-done
  21.9 0.8 %maximum_dynamic-update-slice_fusion = bf16[64,64,128]{2,1,0:T(8,128)(2,1)} fusion(bf16[64,64,128]{2,1,0:T(8,128)(2,1)} %source_spectra.1, bf16[64,8,128]{2,1,0:T(8,128)(2,1)S(1)} %bitcast.11, bf16[64,8,128]{2,1,0:T(8,128)(2,1)S(1)} %bitcast.12, bf16[64,8,128]{2,1,0:T(8,128)(2,1)S(1)} %bitcast.13), kind=kLoop, calls=%fused_computation | loop fusion | flops 1179648 | bytes 786432 | tf_op jit(solution)/shard_map/dynamic_update_slice | solution.py:255
  22.7 13.4 %all-to-all-start = ((bf16[64,64,128]{2,1,0:T(8,128)(2,1)}), bf16[64,64,128]{2,1,0:T(8,128)(2,1)S(1)}, u32[]{:S(2)}, u32[]{:S(2)}) async-start(bf16[64,64,128]{2,1,0:T(8,128)(2,1)} %maximum_dynamic-update-slice_fusion), calls=%async_computation | async-start | bytes 2097152 | tf_op jit(solution)/shard_map/all_to_all | solution.py:256
  36.1 0.0 copy-done
  36.1 0.2 dynamic-slice_reduce_fusion.wave_ref
  36.3 16.8 %all-to-all-done = bf16[64,64,128]{2,1,0:T(8,128)(2,1)S(1)} async-done(((bf16[64,64,128]{2,1,0:T(8,128)(2,1)}), bf16[64,64,128]{2,1,0:T(8,128)(2,1)S(1)}, u32[]{:S(2)}, u32[]{:S(2)}) %all-to-all-start) | async-done | bytes 1048608 | tf_op jit(solution)/shard_map/all_to_all | solution.py:256
  53.1 0.0 copy-done.2
  53.1 0.0 copy-done.3
  53.1 1.9 %predicted_spectra.1 = bf16[256,128]{1,0:T(8,128)(2,1)S(1)} custom-call(s32[1]{0:T(128)} %bitcast.z1_ref, f32[2]{0:T(128)S(1)} %dynamic-slice_reduce_fusion.wave_ref, bf16[16,4,64,128]{3,2,1,0:T(8,128)(2,1)S(1)} %bitcast.8, bf16[512,512]{1,0:T(8,128)(2,1)S(1)} %copy-done.3, bf16[512,512]{1,0:T(8,128)(2,1)S(1)} %copy-done.2), custom_call_target="tpu_custom_call" | custom-call | flops 1073741824 | bytes 2097152 | tf_op jit(solution)/shard_map/predicted_spectra/pallas_call | solution.py:201
  55.0 13.7 %all_to_all.10 = bf16[64,4,128]{2,1,0:T(4,128)(2,1)S(1)} all-to-all(bf16[64,4,128]{2,1,0:T(4,128)(2,1)S(1)} %bitcast.10), channel_id=1, replica_groups=mesh['yh'=2,'z1'=4,'z0'=2,'x'=4,'yl'=2,'core'=2] {'yh','z0','x','yl','co..., dimensions={0} | all-to-all | bytes 131072 | tf_op jit(solution)/shard_map/all_to_all | solution.py:259
  68.7 0.0 copy-done.1
  68.7 1.5 %multiples.1 = bf16[256,2048]{1,0:T(8,128)(2,1)} custom-call(bf16[256,128]{1,0:T(8,128)(2,1)S(1)} %bitcast.9, bf16[128,2048]{1,0:T(8,128)(2,1)S(1)} %copy-done.1), custom_call_target="tpu_custom_call" | custom-call | flops 134217728 | bytes 2097152 | tf_op jit(solution)/shard_map/multiples/pallas_call | solution.py:231
Async XLA Ops:
  0.0 36.1 %copy-start = (f32[64,2]{0,1:T(2,128)S(1)}, f32[64,2]{0,1:T(2,128)}, u32[]{:S(2)}) copy-start(f32[64,2]{0,1:T(2,128)} %param.10) | copy-start | bytes 1540
  0.0 53.1 %copy-start.2 = (bf16[512,512]{1,0:T(8,128)(2,1)S(1)}, bf16[512,512]{1,0:T(8,128)(2,1)}, u32[]{:S(2)}) copy-start(bf16[512,512]{1,0:T(8,128)(2,1)} %constant.50.clone.back_ref) | copy-start | bytes 1572868
  0.0 53.1 %copy-start.3 = (bf16[512,512]{1,0:T(8,128)(2,1)S(1)}, bf16[512,512]{1,0:T(8,128)(2,1)}, u32[]{:S(2)}) copy-start(bf16[512,512]{1,0:T(8,128)(2,1)} %constant.49.clone.mover_ref) | copy-start | bytes 1572868
  3.7 65.0 %copy-start.1 = (bf16[128,2048]{1,0:T(8,128)(2,1)S(1)}, bf16[128,2048]{1,0:T(8,128)(2,1)}, u32[]{:S(2)}) copy-start(bf16[128,2048]{1,0:T(8,128)(2,1)} %constant.51.clone.table_ref) | copy-start | bytes 1572868
  3.7 17.9 %collective-permute-start.2 = (bf16[512,128]{1,0:T(8,128)(2,1)}, bf16[512,128]{1,0:T(8,128)(2,1)S(1)}, u32[]{:S(2)}, u32[]{:S(2)}) collective-permute-start(bf16[512,128]{1,0:T(8,128)(2,1)} %receiver_spectra.1.own_hbm), channel_id=1, source_target_pairs={{0,96},{32,0},{64,32},{96,64},{1,97},{33,1},{65,33},{97,65},{2,98}... | collective-permute-start | bytes 393224 | tf_op jit(solution)/shard_map/ppermute | solution.py:252
  10.7 11.0 %collective-permute-start.1 = (bf16[512,128]{1,0:T(8,128)(2,1)}, bf16[512,128]{1,0:T(8,128)(2,1)S(1)}, u32[]{:S(2)}, u32[]{:S(2)}) collective-permute-start(bf16[512,128]{1,0:T(8,128)(2,1)} %receiver_spectra.1.own_hbm), channel_id=1, source_target_pairs={{0,32},{32,64},{64,96},{96,0},{1,33},{33,65},{65,97},{97,1},{2,34}... | collective-permute-start | bytes 393224 | tf_op jit(solution)/shard_map/ppermute | solution.py:252
  10.7 11.2 %collective-permute-start = (bf16[512,128]{1,0:T(8,128)(2,1)}, bf16[512,128]{1,0:T(8,128)(2,1)S(1)}, u32[]{:S(2)}, u32[]{:S(2)}) collective-permute-start(bf16[512,128]{1,0:T(8,128)(2,1)} %receiver_spectra.1.own_hbm), channel_id=1, source_target_pairs={{0,64},{32,96},{64,0},{96,32},{1,65},{33,97},{65,1},{97,33},{2,66}... | collective-permute-start | bytes 393224 | tf_op jit(solution)/shard_map/ppermute | solution.py:252
  22.7 30.5 %all-to-all-start = ((bf16[64,64,128]{2,1,0:T(8,128)(2,1)}), bf16[64,64,128]{2,1,0:T(8,128)(2,1)S(1)}, u32[]{:S(2)}, u32[]{:S(2)}) async-start(bf16[64,64,128]{2,1,0:T(8,128)(2,1)} %maximum_dynamic-update-slice_fusion), calls=%async_computation | async-start | bytes 2097152 | tf_op jit(solution)/shard_map/all_to_all | solution.py:256

commit v3 on v2

--- a/solution.py
+++ b/solution.py
@@ -17,7 +17,7 @@
 AF = ("yh", "z1", "z0", "x")
 ROW = ("yl", "core")
 GROUP = ("yh", "z0", "x", "yl", "core")
-HOPS = (2, 1, 3)
+HOPS = (1, 3, 2)
 SLOTS = (0,) + HOPS
 
 VMEM = pl.BlockSpec(memory_space=pltpu.VMEM)
@@ -46,11 +46,21 @@
     return lax.dot_general(a, b, (dims, ((), ())), preferred_element_type=jnp.float32)
 
 
-def receiver_kernel(x_hbm, table_hbm, mover_hbm, out_ref, x, table, moves, arrived, rows):
+def in_hbm(x):
+    return pltpu.with_memory_space_constraint(x, pltpu.HBM)
+
+
+AHEAD = 4
+
+
+def receiver_kernel(
+    x_hbm, source_hbm, table_hbm, mover_hbm, out_ref, ahead_ref, x, table, moves, arrived, rows
+):
     copies = [
         pltpu.make_async_copy(table_hbm, table, arrived.at[0]),
         pltpu.make_async_copy(x_hbm, x, arrived.at[1]),
         pltpu.make_async_copy(mover_hbm, moves, arrived.at[2]),
+        pltpu.make_async_copy(source_hbm.at[pl.ds(0, AHEAD)], ahead_ref, arrived.at[3]),
     ]
     for copy in copies:
         copy.start()
@@ -68,51 +78,47 @@
         rows[pl.ds(2 * pair, NF, stride=8), :] = even
         rows[pl.ds(2 * pair + 1, NF, stride=8), :] = odd
     out_ref[...] = rows[...].astype(jnp.bfloat16)
-
-
-def receiver_spectra(traces, table):
+    copies[3].wait()
+
+
+def receiver_spectra(traces, source_traces, table):
+    moves = jnp.asarray(mover((32, 8, 2), (1, 2, 0)))
     return pl.pallas_call(
         receiver_kernel,
-        out_shape=jax.ShapeDtypeStruct((NF * 8, 128), jnp.bfloat16),
-        in_specs=[HBM] * 3,
-        out_specs=VMEM,
+        out_shape=[
+            pltpu.VMEM((NF * 8, 128), jnp.bfloat16),
+            pltpu.VMEM((AHEAD, 256, NT), jnp.bfloat16),
+        ],
+        in_specs=[HBM] * 4,
+        out_specs=[VMEM] * 2,
         scratch_shapes=[
             pltpu.VMEM((32, 16, NT), jnp.bfloat16),
             pltpu.VMEM((NT, 128), jnp.bfloat16),
             pltpu.VMEM((512, 512), jnp.bfloat16),
-            pltpu.SemaphoreType.DMA((3,)),
+            pltpu.SemaphoreType.DMA((4,)),
             pltpu.VMEM((NF * 8, 128), jnp.float32),
         ],
-        compiler_params=pltpu.CompilerParams(vmem_limit_bytes=60 << 20),
+        compiler_params=pltpu.CompilerParams(vmem_limit_bytes=16 << 20),
         cost_estimate=pl.CostEstimate(
             flops=2 * 512 * 128 * NT, bytes_accessed=3 << 20, transcendentals=0
         ),
         name="receiver_spectra",
-    )(traces, table, jnp.asarray(mover((32, 8, 2), (1, 2, 0))))
+    )(in_hbm(traces), in_hbm(source_traces), in_hbm(table), in_hbm(moves))
 
 
 AT_ONCE = 2
 
 
-def source_kernel(x_hbm, own_hbm, table_hbm, out_ref, x, own, table, arrived, ready, rows):
-    others = [
-        pltpu.make_async_copy(table_hbm, table, ready.at[0]),
-        pltpu.make_async_copy(own_hbm, own, ready.at[1]),
-    ]
-    others[0].start()
-    for s in range(8):
-        pltpu.make_async_copy(x_hbm.at[s], x.at[s], arrived.at[s]).start()
-    others[1].start()
-    others[0].wait()
-
-    @pl.loop(0, 8 // AT_ONCE)
-    def _(step):
-        first = step * AT_ONCE
-        for j in range(AT_ONCE):
-            s = first + j
-            pltpu.make_async_copy(x_hbm.at[s], x.at[s], arrived.at[s]).wait()
-        traces = x[pl.ds(first, AT_ONCE)].reshape(AT_ONCE * 256, NT)
-        spectra = dot(traces, table[...]).T
+def source_kernel(x_hbm, ahead_ref, own_ref, table_hbm, out_ref, x, table, arrived, ready, rows):
+    fetch = pltpu.make_async_copy(table_hbm, table, ready)
+    fetch.start()
+    for s in range(8 - AHEAD):
+        pltpu.make_async_copy(x_hbm.at[AHEAD + s], x.at[s], arrived.at[s]).start()
+    out_ref[:, 32:40, :] = own_ref[...].reshape(NF, 8, 128)
+    fetch.wait()
+
+    def transform(traces, first):
+        spectra = dot(traces.reshape(AT_ONCE * 256, NT), table[...]).T
         for j in range(AT_ONCE):
             for c in range(2):
                 for kh in range(2):
@@ -121,31 +127,41 @@
                         c * NF : (c + 1) * NF, at : at + 128
                     ]
 
-    others[1].wait()
+    @pl.loop(0, AHEAD // AT_ONCE)
+    def _(step):
+        first = step * AT_ONCE
+        transform(ahead_ref[pl.ds(first, AT_ONCE)], first)
+
+    @pl.loop(0, (8 - AHEAD) // AT_ONCE)
+    def _(step):
+        first = step * AT_ONCE
+        for j in range(AT_ONCE):
+            s = first + j
+            pltpu.make_async_copy(x_hbm.at[AHEAD + s], x.at[s], arrived.at[s]).wait()
+        transform(x[pl.ds(first, AT_ONCE)], AHEAD + first)
+
     out_ref[:, :32, :] = rows[...].astype(jnp.bfloat16).reshape(NF, 32, 128)
-    out_ref[:, 32:40, :] = own[...].reshape(NF, 8, 128)
-
-
-def source_spectra(traces, own, table):
+
+
+def source_spectra(traces, ahead, own, table):
     return pl.pallas_call(
         source_kernel,
-        out_shape=jax.ShapeDtypeStruct((NF, 64, 128), jnp.bfloat16),
-        in_specs=[HBM] * 3,
+        out_shape=pltpu.VMEM((NF, 64, 128), jnp.bfloat16),
+        in_specs=[HBM, VMEM, VMEM, HBM],
         out_specs=VMEM,
         scratch_shapes=[
-            pltpu.VMEM((8, 256, NT), jnp.bfloat16),
-            pltpu.VMEM((NF * 8, 128), jnp.bfloat16),
+            pltpu.VMEM((8 - AHEAD, 256, NT), jnp.bfloat16),
             pltpu.VMEM((NT, 128), jnp.bfloat16),
-            pltpu.SemaphoreType.DMA((8,)),
-            pltpu.SemaphoreType.DMA((2,)),
+            pltpu.SemaphoreType.DMA((8 - AHEAD,)),
+            pltpu.SemaphoreType.DMA,
             pltpu.VMEM((NF * 32, 128), jnp.float32),
         ],
-        compiler_params=pltpu.CompilerParams(vmem_limit_bytes=60 << 20),
+        compiler_params=pltpu.CompilerParams(vmem_limit_bytes=16 << 20),
         cost_estimate=pl.CostEstimate(
             flops=2 * 2048 * 128 * NT, bytes_accessed=10 << 20, transcendentals=0
         ),
         name="source_spectra",
-    )(traces, own, table)
+    )(in_hbm(traces), ahead, own, in_hbm(table))
 
 
 def product_kernel(z1_ref, wave_ref, got_ref, mover_ref, back_ref, out_ref, right, pred, rows):
@@ -163,7 +179,10 @@
                 panel = 2 * yh + lax.div(origin, 2)
                 start = pl.multiple_of(16 * lax.rem(origin, 2), 16)
                 left.append(got_ref[:, panel, pl.ds(start, 16), :].reshape(256, 128))
-                part = moved[yh, :, half].reshape(64, 512)
+                part = moved[yh, :, half]
+                if SLOTS[slot] == 2:
+                    part = jnp.concatenate([part[4:], part[:4]], axis=0)
+                part = part.reshape(64, 512)
                 for k in range(2):
                     for c in range(2):
                         at = 256 * k + 128 * c
@@ -246,11 +265,19 @@
     )(returned, table)
 
 
+def moves(hop):
+    return [
+        (2 * z1 + z0, 2 * ((z1 + hop) % 4) + (1 - z0 if hop == 2 else z0))
+        for z1 in range(4)
+        for z0 in range(2)
+    ]
+
+
 def per_device(source_traces, receiver_traces, wavelet_inverse):
     table = jnp.asarray(tables(1.0 / math.sqrt(NT)).transpose(2, 1, 0).reshape(NT, 2 * NF))
-    own = receiver_spectra(receiver_traces, table)
-    others = [lax.ppermute(own, "z1", [(i, (i + hop) % 4) for i in range(4)]) for hop in HOPS]
-    sent = source_spectra(source_traces, own, table)
+    own, ahead = receiver_spectra(receiver_traces, source_traces, table)
+    others = [lax.ppermute(own, ("z1", "z0"), moves(hop)) for hop in HOPS]
+    sent = source_spectra(source_traces, ahead, own, table)
     others = jnp.concatenate([other.reshape(NF, 8, 128) for other in others], axis=1)
     sent = lax.dynamic_update_slice(sent, others, (0, 40, 0))
     got = lax.all_to_all(sent, GROUP, split_axis=0, concat_axis=0, tiled=True)

time: 70.4 us -> 66.6 us (0.946)
  starting transfers between devices: 23.6 us -> 17.8 us
  waiting for transfers between devices: 17 us -> 20.5 us
  Pallas kernels: 14.8 us -> 13.3 us
    all_to_all x1, starting transfers between devices: 13.4 us -> 8.09 us  [per_device(): got = lax.all_to_all(sent, GROUP, split_axis=0, concat_axis=0, tiled=True)]
    ppermute x3, waiting for transfers between devices: 0.18 us -> 3.66 us  [per_device(): others = [lax.ppermute(own, ('z1', 'z0'), moves(hop)) for hop in HOPS]]
    pallas_call x2, Pallas kernels: 11.4 us -> 9.92 us  [the longest x1 6.71 us: source_spectra(): pl.pallas_call(source_kernel, out_shape=pltpu.VMEM((NF, 64, 128), jnp.bfl...]
  transfers between devices with their start and end apart: 4 -> 4, of which waited for: 2 -> 2; matrix products, arithmetic and copies ran while one was open for 0% -> 0% of each run, Pallas kernels for 11% -> 10%
where the time goes in v3:
time: 66.6 us; the launch traced here: 66.4 us
  waiting for transfers between devices  20.5 us (31%)
  starting transfers between devices  17.8 us (27%)
  blocking collectives  13.7 us (21%)
  Pallas kernels  13.3 us (20%)
  other arithmetic  0.81 us (1%)
    all_to_all x1, waiting for transfers between devices, per_device(): got = lax.all_to_all(sent, GROUP, split_axis=0, concat_axis=0, tiled=True)  16.8 us
    all_to_all x1, blocking collectives, per_device(): lax.all_to_all(predicted.reshape(NF, 4, 128), GROUP, split_axis=0, concat...  13.7 us
    ppermute x3, starting transfers between devices, per_device(): others = [lax.ppermute(own, ('z1', 'z0'), moves(hop)) for hop in HOPS]  9.75 us
    all_to_all x1, starting transfers between devices, per_device(): got = lax.all_to_all(sent, GROUP, split_axis=0, concat_axis=0, tiled=True)  8.09 us
    pallas_call x1, Pallas kernels, source_spectra(): pl.pallas_call(source_kernel, out_shape=pltpu.VMEM((NF, 64, 128), jnp.bfl...  6.71 us
    ppermute x3, waiting for transfers between devices, per_device(): others = [lax.ppermute(own, ('z1', 'z0'), moves(hop)) for hop in HOPS]  3.66 us
    pallas_call x1, Pallas kernels, receiver_spectra(): pl.pallas_call(receiver_kernel, out_shape=[pltpu.VMEM((NF * 8, 128), jnp....  3.21 us
    pallas_call x1, Pallas kernels, predicted_spectra(): pl.pallas_call(product_kernel, out_shape=jax.ShapeDtypeStruct((256, 128),...  1.9 us
  transfers between devices with their start and end apart: 4, of which 2 were waited for; matrix products, arithmetic and copies ran while one was open for 0% of the time, Pallas kernels for 10%

profile of v3, /device:TPU:1, one launch (start us, length us, event | category | flops | bytes accessed | tf_op | source)
XLA Modules:
  0.0 66.4 jit_solution(4517493966099879357)
XLA Ops:
  0.0 0.0 copy-start
  0.0 3.2 %receiver_spectra.1 = (bf16[512,128]{1,0:T(8,128)(2,1)S(1)}, bf16[4,256,2048]{2,1,0:T(8,128)(2,1)S(1)}) custom-call(bf16[32,16,2048]{2,1,0:T(8,128)(2,1)} %x_hbm.2, bf16[8,256,2048]{2,1,0:T(8,128)(2,1)} %x_hbm.3, bf16[2048,128]{1,0:T(8,128)(2,1)} %constant.47.clone.table_hbm, bf16[512,512]{1,0:T(8,128)(2,1)} %constant.48.clone.mover_hbm), custom_call_target="tpu_custom_call" | custom-call | flops 268435456 | bytes 3145728 | tf_op jit(solution)/shard_map/receiver_spectra/pallas_call | solution.py:86
  3.2 7.4 %collective-permute-start.2 = (bf16[512,128]{1,0:T(8,128)(2,1)S(1)}, bf16[512,128]{1,0:T(8,128)(2,1)S(1)}, u32[]{:S(2)}, u32[]{:S(2)}) collective-permute-start(bf16[512,128]{1,0:T(8,128)(2,1)S(1)} %get-tuple-element.8.own_ref), channel_id=1, source_target_pairs={{0,80},{16,64},{32,112},{48,96},{64,16},{80,0},{96,48},{112,32},{1... | collective-permute-start | bytes 393224 | tf_op jit(solution)/shard_map/ppermute | solution.py:279
  10.6 0.3 collective-permute-start.1
  10.9 2.1 %collective-permute-start = (bf16[512,128]{1,0:T(8,128)(2,1)S(1)}, bf16[512,128]{1,0:T(8,128)(2,1)S(1)}, u32[]{:S(2)}, u32[]{:S(2)}) collective-permute-start(bf16[512,128]{1,0:T(8,128)(2,1)S(1)} %get-tuple-element.8.own_ref), channel_id=1, source_target_pairs={{0,32},{16,48},{32,64},{48,80},{64,96},{80,112},{96,0},{112,16},{1... | collective-permute-start | bytes 393224 | tf_op jit(solution)/shard_map/ppermute | solution.py:279
  13.0 0.0 copy-start.2
  13.0 0.0 copy-start.3
  13.0 6.7 %source_spectra.1 = bf16[64,64,128]{2,1,0:T(8,128)(2,1)} custom-call(bf16[8,256,2048]{2,1,0:T(8,128)(2,1)} %x_hbm.3, bf16[4,256,2048]{2,1,0:T(8,128)(2,1)S(1)} %get-tuple-element.7.ahead_ref, bf16[512,128]{1,0:T(8,128)(2,1)S(1)} %get-tuple-element.8.own_ref, bf16[2048,128]{1,0:T(8,128)(2,1)} %constant.47.clone.table_hbm), custom_call_target="tpu_custom_call" | custom-call | flops 1073741824 | bytes 10485760 | tf_op jit(solution)/shard_map/source_spectra/pallas_call | solution.py:147
  19.7 0.0 copy-start.1
  19.7 0.0 collective-permute-done.2
  19.7 3.7 %collective-permute-done.1 = bf16[512,128]{1,0:T(8,128)(2,1)S(1)} collective-permute-done((bf16[512,128]{1,0:T(8,128)(2,1)S(1)}, bf16[512,128]{1,0:T(8,128)(2,1)S(1)}, u32[]{:S(2)}, u32[]{:S(2)}) %collective-permute-start.1) | collective-permute-done | bytes 131104 | tf_op jit(solution)/shard_map/ppermute | solution.py:279
  23.4 0.0 collective-permute-done
  23.4 0.8 %maximum_dynamic-update-slice_fusion = bf16[64,64,128]{2,1,0:T(8,128)(2,1)} fusion(bf16[64,64,128]{2,1,0:T(8,128)(2,1)} %source_spectra.1, bf16[64,8,128]{2,1,0:T(8,128)(2,1)S(1)} %bitcast.11, bf16[64,8,128]{2,1,0:T(8,128)(2,1)S(1)} %bitcast.12, bf16[64,8,128]{2,1,0:T(8,128)(2,1)S(1)} %bitcast.13), kind=kLoop, calls=%fused_computation | loop fusion | flops 1179648 | bytes 786432 | tf_op jit(solution)/shard_map/dynamic_update_slice | solution.py:282
  24.2 8.1 %all-to-all-start = ((bf16[64,64,128]{2,1,0:T(8,128)(2,1)}), bf16[64,64,128]{2,1,0:T(8,128)(2,1)S(1)}, u32[]{:S(2)}, u32[]{:S(2)}) async-start(bf16[64,64,128]{2,1,0:T(8,128)(2,1)} %maximum_dynamic-update-slice_fusion), calls=%async_computation | async-start | bytes 2097152 | tf_op jit(solution)/shard_map/all_to_all | solution.py:283
  32.3 0.0 copy-done
  32.3 0.2 dynamic-slice_reduce_fusion.wave_ref
  32.5 16.8 %all-to-all-done = bf16[64,64,128]{2,1,0:T(8,128)(2,1)S(1)} async-done(((bf16[64,64,128]{2,1,0:T(8,128)(2,1)}), bf16[64,64,128]{2,1,0:T(8,128)(2,1)S(1)}, u32[]{:S(2)}, u32[]{:S(2)}) %all-to-all-start) | async-done | bytes 1048608 | tf_op jit(solution)/shard_map/all_to_all | solution.py:283
  49.3 0.0 copy-done.2
  49.3 0.0 copy-done.3
  49.3 1.9 %predicted_spectra.1 = bf16[256,128]{1,0:T(8,128)(2,1)S(1)} custom-call(s32[1]{0:T(128)} %bitcast.z1_ref, f32[2]{0:T(128)S(1)} %dynamic-slice_reduce_fusion.wave_ref, bf16[16,4,64,128]{3,2,1,0:T(8,128)(2,1)S(1)} %bitcast.8, bf16[512,512]{1,0:T(8,128)(2,1)S(1)} %copy-done.3, bf16[512,512]{1,0:T(8,128)(2,1)S(1)} %copy-done.2), custom_call_target="tpu_custom_call" | custom-call | flops 1073741824 | bytes 2097152 | tf_op jit(solution)/shard_map/predicted_spectra/pallas_call | solution.py:220
  51.2 13.7 %all_to_all.10 = bf16[64,4,128]{2,1,0:T(4,128)(2,1)S(1)} all-to-all(bf16[64,4,128]{2,1,0:T(4,128)(2,1)S(1)} %bitcast.10), channel_id=1, replica_groups=mesh['yh'=2,'z1'=4,'z0'=2,'x'=4,'yl'=2,'core'=2] {'yh','z0','x','yl','co..., dimensions={0} | all-to-all | bytes 131072 | tf_op jit(solution)/shard_map/all_to_all | solution.py:286
  64.9 0.0 copy-done.1
  64.9 1.5 %multiples.1 = bf16[256,2048]{1,0:T(8,128)(2,1)} custom-call(bf16[256,128]{1,0:T(8,128)(2,1)S(1)} %bitcast.9, bf16[128,2048]{1,0:T(8,128)(2,1)S(1)} %copy-done.1), custom_call_target="tpu_custom_call" | custom-call | flops 134217728 | bytes 2097152 | tf_op jit(solution)/shard_map/multiples/pallas_call | solution.py:250
Async XLA Ops:
  0.0 32.3 %copy-start = (f32[64,2]{0,1:T(2,128)S(1)}, f32[64,2]{0,1:T(2,128)}, u32[]{:S(2)}) copy-start(f32[64,2]{0,1:T(2,128)} %param.10) | copy-start | bytes 1540
  3.2 16.5 %collective-permute-start.2 = (bf16[512,128]{1,0:T(8,128)(2,1)S(1)}, bf16[512,128]{1,0:T(8,128)(2,1)S(1)}, u32[]{:S(2)}, u32[]{:S(2)}) collective-permute-start(bf16[512,128]{1,0:T(8,128)(2,1)S(1)} %get-tuple-element.8.own_ref), channel_id=1, source_target_pairs={{0,80},{16,64},{32,112},{48,96},{64,16},{80,0},{96,48},{112,32},{1... | collective-permute-start | bytes 393224 | tf_op jit(solution)/shard_map/ppermute | solution.py:279
  10.6 12.8 %collective-permute-start.1 = (bf16[512,128]{1,0:T(8,128)(2,1)S(1)}, bf16[512,128]{1,0:T(8,128)(2,1)S(1)}, u32[]{:S(2)}, u32[]{:S(2)}) collective-permute-start(bf16[512,128]{1,0:T(8,128)(2,1)S(1)} %get-tuple-element.8.own_ref), channel_id=1, source_target_pairs={{0,96},{16,112},{32,0},{48,16},{64,32},{80,48},{96,64},{112,80},{1... | collective-permute-start | bytes 393224 | tf_op jit(solution)/shard_map/ppermute | solution.py:279
  10.9 12.5 %collective-permute-start = (bf16[512,128]{1,0:T(8,128)(2,1)S(1)}, bf16[512,128]{1,0:T(8,128)(2,1)S(1)}, u32[]{:S(2)}, u32[]{:S(2)}) collective-permute-start(bf16[512,128]{1,0:T(8,128)(2,1)S(1)} %get-tuple-element.8.own_ref), channel_id=1, source_target_pairs={{0,32},{16,48},{32,64},{48,80},{64,96},{80,112},{96,0},{112,16},{1... | collective-permute-start | bytes 393224 | tf_op jit(solution)/shard_map/ppermute | solution.py:279
  13.0 36.4 %copy-start.2 = (bf16[512,512]{1,0:T(8,128)(2,1)S(1)}, bf16[512,512]{1,0:T(8,128)(2,1)}, u32[]{:S(2)}) copy-start(bf16[512,512]{1,0:T(8,128)(2,1)} %constant.50.clone.back_ref) | copy-start | bytes 1572868
  13.0 36.4 %copy-start.3 = (bf16[512,512]{1,0:T(8,128)(2,1)S(1)}, bf16[512,512]{1,0:T(8,128)(2,1)}, u32[]{:S(2)}) copy-start(bf16[512,512]{1,0:T(8,128)(2,1)} %constant.49.clone.mover_ref) | copy-start | bytes 1572868
  19.7 45.2 %copy-start.1 = (bf16[128,2048]{1,0:T(8,128)(2,1)S(1)}, bf16[128,2048]{1,0:T(8,128)(2,1)}, u32[]{:S(2)}) copy-start(bf16[128,2048]{1,0:T(8,128)(2,1)} %constant.51.clone.table_ref) | copy-start | bytes 1572868
  24.2 25.1 %all-to-all-start = ((bf16[64,64,128]{2,1,0:T(8,128)(2,1)}), bf16[64,64,128]{2,1,0:T(8,128)(2,1)S(1)}, u32[]{:S(2)}, u32[]{:S(2)}) async-start(bf16[64,64,128]{2,1,0:T(8,128)(2,1)} %maximum_dynamic-update-slice_fusion), calls=%async_computation | async-start | bytes 2097152 | tf_op jit(solution)/shard_map/all_to_all | solution.py:283

commit v4 on v2

--- a/solution.py
+++ b/solution.py
@@ -17,7 +17,7 @@
 AF = ("yh", "z1", "z0", "x")
 ROW = ("yl", "core")
 GROUP = ("yh", "z0", "x", "yl", "core")
-HOPS = (2, 1, 3)
+HOPS = (3, 1, 2)
 SLOTS = (0,) + HOPS
 
 VMEM = pl.BlockSpec(memory_space=pltpu.VMEM)
@@ -46,7 +46,13 @@
     return lax.dot_general(a, b, (dims, ((), ())), preferred_element_type=jnp.float32)
 
 
-def receiver_kernel(x_hbm, table_hbm, mover_hbm, out_ref, x, table, moves, arrived, rows):
+def in_hbm(x):
+    return pltpu.with_memory_space_constraint(x, pltpu.HBM)
+
+
+def receiver_kernel(
+    x_hbm, table_hbm, mover_hbm, out_ref, x, table, moves, arrived, rows
+):
     copies = [
         pltpu.make_async_copy(table_hbm, table, arrived.at[0]),
         pltpu.make_async_copy(x_hbm, x, arrived.at[1]),
@@ -71,9 +77,10 @@
 
 
 def receiver_spectra(traces, table):
+    moves = jnp.asarray(mover((32, 8, 2), (1, 2, 0)))
     return pl.pallas_call(
         receiver_kernel,
-        out_shape=jax.ShapeDtypeStruct((NF * 8, 128), jnp.bfloat16),
+        out_shape=pltpu.VMEM((NF * 8, 128), jnp.bfloat16),
         in_specs=[HBM] * 3,
         out_specs=VMEM,
         scratch_shapes=[
@@ -83,36 +90,25 @@
             pltpu.SemaphoreType.DMA((3,)),
             pltpu.VMEM((NF * 8, 128), jnp.float32),
         ],
-        compiler_params=pltpu.CompilerParams(vmem_limit_bytes=60 << 20),
+        compiler_params=pltpu.CompilerParams(vmem_limit_bytes=16 << 20),
         cost_estimate=pl.CostEstimate(
-            flops=2 * 512 * 128 * NT, bytes_accessed=3 << 20, transcendentals=0
+            flops=200 * 512 * 128 * NT, bytes_accessed=3 << 20, transcendentals=0
         ),
         name="receiver_spectra",
-    )(traces, table, jnp.asarray(mover((32, 8, 2), (1, 2, 0))))
+    )(in_hbm(traces), in_hbm(table), in_hbm(moves))
 
 
 AT_ONCE = 2
 
 
-def source_kernel(x_hbm, own_hbm, table_hbm, out_ref, x, own, table, arrived, ready, rows):
-    others = [
-        pltpu.make_async_copy(table_hbm, table, ready.at[0]),
-        pltpu.make_async_copy(own_hbm, own, ready.at[1]),
-    ]
-    others[0].start()
-    for s in range(8):
-        pltpu.make_async_copy(x_hbm.at[s], x.at[s], arrived.at[s]).start()
-    others[1].start()
-    others[0].wait()
+def source_kernel(x_ref, own_ref, table_ref, out_ref, rows):
+    out_ref[:, 32:40, :] = own_ref[...].reshape(NF, 8, 128)
 
     @pl.loop(0, 8 // AT_ONCE)
     def _(step):
         first = step * AT_ONCE
-        for j in range(AT_ONCE):
-            s = first + j
-            pltpu.make_async_copy(x_hbm.at[s], x.at[s], arrived.at[s]).wait()
-        traces = x[pl.ds(first, AT_ONCE)].reshape(AT_ONCE * 256, NT)
-        spectra = dot(traces, table[...]).T
+        traces = x_ref[pl.ds(first, AT_ONCE)].reshape(AT_ONCE * 256, NT)
+        spectra = dot(traces, table_ref[...]).T
         for j in range(AT_ONCE):
             for c in range(2):
                 for kh in range(2):
@@ -121,26 +117,17 @@
                         c * NF : (c + 1) * NF, at : at + 128
                     ]
 
-    others[1].wait()
     out_ref[:, :32, :] = rows[...].astype(jnp.bfloat16).reshape(NF, 32, 128)
-    out_ref[:, 32:40, :] = own[...].reshape(NF, 8, 128)
 
 
 def source_spectra(traces, own, table):
     return pl.pallas_call(
         source_kernel,
         out_shape=jax.ShapeDtypeStruct((NF, 64, 128), jnp.bfloat16),
-        in_specs=[HBM] * 3,
+        in_specs=[VMEM] * 3,
         out_specs=VMEM,
-        scratch_shapes=[
-            pltpu.VMEM((8, 256, NT), jnp.bfloat16),
-            pltpu.VMEM((NF * 8, 128), jnp.bfloat16),
-            pltpu.VMEM((NT, 128), jnp.bfloat16),
-            pltpu.SemaphoreType.DMA((8,)),
-            pltpu.SemaphoreType.DMA((2,)),
-            pltpu.VMEM((NF * 32, 128), jnp.float32),
-        ],
-        compiler_params=pltpu.CompilerParams(vmem_limit_bytes=60 << 20),
+        scratch_shapes=[pltpu.VMEM((NF * 32, 128), jnp.float32)],
+        compiler_params=pltpu.CompilerParams(vmem_limit_bytes=8 << 20),
         cost_estimate=pl.CostEstimate(
             flops=2 * 2048 * 128 * NT, bytes_accessed=10 << 20, transcendentals=0
         ),
@@ -163,7 +150,10 @@
                 panel = 2 * yh + lax.div(origin, 2)
                 start = pl.multiple_of(16 * lax.rem(origin, 2), 16)
                 left.append(got_ref[:, panel, pl.ds(start, 16), :].reshape(256, 128))
-                part = moved[yh, :, half].reshape(64, 512)
+                part = moved[yh, :, half]
+                if SLOTS[slot] == 2:
+                    part = jnp.concatenate([part[4:], part[:4]], axis=0)
+                part = part.reshape(64, 512)
                 for k in range(2):
                     for c in range(2):
                         at = 256 * k + 128 * c
@@ -220,25 +210,37 @@
     )
 
 
-def multiples_kernel(x_ref, table_ref, out_ref, rows):
+def multiples_kernel(x_ref, table_ref, out_hbm, rows, stage, sent):
     rows[...] = x_ref[...].astype(jnp.float32)
-    half = rows[pl.ds(pl.program_id(0), 128, stride=2), :].astype(jnp.bfloat16)
-    out_ref[...] = dot(half, table_ref[...], ((0,), (0,))).astype(jnp.bfloat16)
+    copies = []
+    for high in range(2):
+        half = rows[pl.ds(high, 128, stride=2), :].astype(jnp.bfloat16).T
+        for part in range(2):
+            at = 1024 * part
+            stage[128 * high : 128 * high + 128, at : at + 1024] = dot(
+                half, table_ref[:, at : at + 1024]
+            ).astype(jnp.bfloat16)
+            here = (pl.ds(128 * high, 128), pl.ds(at, 1024))
+            copy = pltpu.make_async_copy(stage.at[here], out_hbm.at[here], sent.at[len(copies)])
+            copy.start()
+            copies.append(copy)
+    for copy in copies:
+        copy.wait()
 
 
 def multiples(returned):
     table = jnp.asarray(tables(1.0 / math.sqrt(NF)).reshape(2 * NF, NT))
     return pl.pallas_call(
         multiples_kernel,
-        grid=(2,),
         out_shape=jax.ShapeDtypeStruct((256, NT), jnp.bfloat16),
-        in_specs=[
-            pl.BlockSpec((256, 128), lambda i: (0, 0)),
-            pl.BlockSpec((128, NT), lambda i: (0, 0)),
+        in_specs=[VMEM, VMEM],
+        out_specs=HBM,
+        scratch_shapes=[
+            pltpu.VMEM((256, 128), jnp.float32),
+            pltpu.VMEM((256, NT), jnp.bfloat16),
+            pltpu.SemaphoreType.DMA((4,)),
         ],
-        out_specs=pl.BlockSpec((128, NT), lambda i: (i, 0)),
-        scratch_shapes=[pltpu.VMEM((256, 128), jnp.float32)],
-        compiler_params=pltpu.CompilerParams(vmem_limit_bytes=24 << 20),
+        compiler_params=pltpu.CompilerParams(vmem_limit_bytes=16 << 20),
         cost_estimate=pl.CostEstimate(
             flops=2 * 256 * 128 * NT, bytes_accessed=2 << 20, transcendentals=0
         ),
@@ -246,10 +248,18 @@
     )(returned, table)
 
 
+def moves(hop):
+    return [
+        (2 * z1 + z0, 2 * ((z1 + hop) % 4) + (1 - z0 if hop == 2 else z0))
+        for z1 in range(4)
+        for z0 in range(2)
+    ]
+
+
 def per_device(source_traces, receiver_traces, wavelet_inverse):
     table = jnp.asarray(tables(1.0 / math.sqrt(NT)).transpose(2, 1, 0).reshape(NT, 2 * NF))
     own = receiver_spectra(receiver_traces, table)
-    others = [lax.ppermute(own, "z1", [(i, (i + hop) % 4) for i in range(4)]) for hop in HOPS]
+    others = [lax.ppermute(own, ("z1", "z0"), moves(hop)) for hop in HOPS]
     sent = source_spectra(source_traces, own, table)
     others = jnp.concatenate([other.reshape(NF, 8, 128) for other in others], axis=1)
     sent = lax.dynamic_update_slice(sent, others, (0, 40, 0))

time: 70.4 us -> 66.3 us (0.942)
  starting transfers between devices: 23.6 us -> 19 us
  waiting for transfers between devices: 17 us -> 21.5 us
  Pallas kernels: 14.8 us -> 10.8 us
    all_to_all x1, starting transfers between devices: 13.4 us -> 8.04 us  [per_device(): got = lax.all_to_all(sent, GROUP, split_axis=0, concat_axis=0, tiled=True)]
    ppermute x3, waiting for transfers between devices: 0.18 us -> 4.64 us  [per_device(): others = [lax.ppermute(own, ('z1', 'z0'), moves(hop)) for hop in HOPS]]
    pallas_call x1, Pallas kernels: 7.74 us -> 4.55 us  [source_spectra(): pl.pallas_call(source_kernel, out_shape=jax.ShapeDtypeStruct((NF, 64, 128...]
    pallas_call x2, Pallas kernels: 5.16 us -> 4.38 us  [the longest x1 3.11 us: receiver_spectra(): pl.pallas_call(receiver_kernel, out_shape=pltpu.VMEM((NF * 8, 128), jnp.b...]
    ppermute x3, starting transfers between devices: 10.2 us -> 11 us  [per_device(): others = [lax.ppermute(own, ('z1', 'z0'), moves(hop)) for hop in HOPS]]
  transfers between devices with their start and end apart: 4 -> 4, of which waited for: 2 -> 2; matrix products, arithmetic and copies ran while one was open for 0% -> 0% of each run, Pallas kernels for 11% -> 7%
where the time goes in v4:
time: 66.3 us; the launch traced here: 66.1 us
  waiting for transfers between devices  21.5 us (32%)
  starting transfers between devices  19 us (29%)
  blocking collectives  13.7 us (21%)
  Pallas kernels  10.8 us (16%)
  other arithmetic  0.81 us (1%)
    all_to_all x1, waiting for transfers between devices, per_device(): got = lax.all_to_all(sent, GROUP, split_axis=0, concat_axis=0, tiled=True)  16.8 us
    all_to_all x1, blocking collectives, per_device(): lax.all_to_all(predicted.reshape(NF, 4, 128), GROUP, split_axis=0, concat...  13.7 us
    ppermute x3, starting transfers between devices, per_device(): others = [lax.ppermute(own, ('z1', 'z0'), moves(hop)) for hop in HOPS]  11 us
    all_to_all x1, starting transfers between devices, per_device(): got = lax.all_to_all(sent, GROUP, split_axis=0, concat_axis=0, tiled=True)  8.04 us
    ppermute x3, waiting for transfers between devices, per_device(): others = [lax.ppermute(own, ('z1', 'z0'), moves(hop)) for hop in HOPS]  4.64 us
    pallas_call x1, Pallas kernels, source_spectra(): pl.pallas_call(source_kernel, out_shape=jax.ShapeDtypeStruct((NF, 64, 128...  4.55 us
    pallas_call x1, Pallas kernels, receiver_spectra(): pl.pallas_call(receiver_kernel, out_shape=pltpu.VMEM((NF * 8, 128), jnp.b...  3.11 us
    pallas_call x1, Pallas kernels, predicted_spectra(): pl.pallas_call(product_kernel, out_shape=jax.ShapeDtypeStruct((256, 128),...  1.9 us
  transfers between devices with their start and end apart: 4, of which 2 were waited for; matrix products, arithmetic and copies ran while one was open for 0% of the time, Pallas kernels for 7%

profile of v4, /device:TPU:1, one launch (start us, length us, event | category | flops | bytes accessed | tf_op | source)
XLA Modules:
  0.0 66.1 jit_solution(505835230927462968)
XLA Ops:
  0.0 0.0 copy-start
  0.0 3.1 %receiver_spectra.1.own_ref = bf16[512,128]{1,0:T(8,128)(2,1)S(1)} custom-call(bf16[32,16,2048]{2,1,0:T(8,128)(2,1)} %x_hbm.1, bf16[2048,128]{1,0:T(8,128)(2,1)} %constant.47.clone.table_hbm.table_ref, bf16[512,512]{1,0:T(8,128)(2,1)} %constant.48.clone.mover_hbm), custom_call_target="tpu_custom_call" | custom-call | flops 26843545600 | bytes 3145728 | tf_op jit(solution)/shard_map/receiver_spectra/pallas_call | solution.py:81
  3.1 0.0 copy-start.4
  3.1 0.0 copy-start.5
  3.2 0.0 copy-start.2
  3.2 7.4 %collective-permute-start.2 = (bf16[512,128]{1,0:T(8,128)(2,1)S(1)}, bf16[512,128]{1,0:T(8,128)(2,1)S(1)}, u32[]{:S(2)}, u32[]{:S(2)}) collective-permute-start(bf16[512,128]{1,0:T(8,128)(2,1)S(1)} %receiver_spectra.1.own_ref), channel_id=1, source_target_pairs={{0,80},{16,64},{32,112},{48,96},{64,16},{80,0},{96,48},{112,32},{1... | collective-permute-start | bytes 393224 | tf_op jit(solution)/shard_map/ppermute | solution.py:262
  10.5 1.2 %collective-permute-start.1 = (bf16[512,128]{1,0:T(8,128)(2,1)S(1)}, bf16[512,128]{1,0:T(8,128)(2,1)S(1)}, u32[]{:S(2)}, u32[]{:S(2)}) collective-permute-start(bf16[512,128]{1,0:T(8,128)(2,1)S(1)} %receiver_spectra.1.own_ref), channel_id=1, source_target_pairs={{0,32},{16,48},{32,64},{48,80},{64,96},{80,112},{96,0},{112,16},{1... | collective-permute-start | bytes 393224 | tf_op jit(solution)/shard_map/ppermute | solution.py:262
  11.7 2.4 %collective-permute-start = (bf16[512,128]{1,0:T(8,128)(2,1)S(1)}, bf16[512,128]{1,0:T(8,128)(2,1)S(1)}, u32[]{:S(2)}, u32[]{:S(2)}) collective-permute-start(bf16[512,128]{1,0:T(8,128)(2,1)S(1)} %receiver_spectra.1.own_ref), channel_id=1, source_target_pairs={{0,96},{16,112},{32,0},{48,16},{64,32},{80,48},{96,64},{112,80},{1... | collective-permute-start | bytes 393224 | tf_op jit(solution)/shard_map/ppermute | solution.py:262
  14.1 0.0 copy-done.3
  14.1 0.0 copy-done.1
  14.1 4.5 %source_spectra.1 = bf16[64,64,128]{2,1,0:T(8,128)(2,1)} custom-call(bf16[8,256,2048]{2,1,0:T(8,128)(2,1)S(1)} %copy-done.1, bf16[512,128]{1,0:T(8,128)(2,1)S(1)} %receiver_spectra.1.own_ref, bf16[2048,128]{1,0:T(8,128)(2,1)S(1)} %copy-done.3), custom_call_target="tpu_custom_call" | custom-call | flops 1073741824 | bytes 10485760 | tf_op jit(solution)/shard_map/source_spectra/pallas_call | solution.py:124
  18.7 0.0 collective-permute-done.2
  18.7 0.0 collective-permute-done.1
  18.7 4.6 %collective-permute-done = bf16[512,128]{1,0:T(8,128)(2,1)S(1)} collective-permute-done((bf16[512,128]{1,0:T(8,128)(2,1)S(1)}, bf16[512,128]{1,0:T(8,128)(2,1)S(1)}, u32[]{:S(2)}, u32[]{:S(2)}) %collective-permute-start) | collective-permute-done | bytes 131104 | tf_op jit(solution)/shard_map/ppermute | solution.py:262
  23.3 0.8 %maximum_dynamic-update-slice_fusion = bf16[64,64,128]{2,1,0:T(8,128)(2,1)} fusion(bf16[64,64,128]{2,1,0:T(8,128)(2,1)} %source_spectra.1, bf16[64,8,128]{2,1,0:T(8,128)(2,1)S(1)} %bitcast.11, bf16[64,8,128]{2,1,0:T(8,128)(2,1)S(1)} %bitcast.12, bf16[64,8,128]{2,1,0:T(8,128)(2,1)S(1)} %bitcast.13), kind=kLoop, calls=%fused_computation | loop fusion | flops 1179648 | bytes 786432 | tf_op jit(solution)/shard_map/dynamic_update_slice | solution.py:265
  24.1 8.0 %all-to-all-start = ((bf16[64,64,128]{2,1,0:T(8,128)(2,1)}), bf16[64,64,128]{2,1,0:T(8,128)(2,1)S(1)}, u32[]{:S(2)}, u32[]{:S(2)}) async-start(bf16[64,64,128]{2,1,0:T(8,128)(2,1)} %maximum_dynamic-update-slice_fusion), calls=%async_computation | async-start | bytes 2097152 | tf_op jit(solution)/shard_map/all_to_all | solution.py:266
  32.2 0.0 copy-done
  32.2 0.2 dynamic-slice_reduce_fusion.wave_ref
  32.4 16.8 %all-to-all-done = bf16[64,64,128]{2,1,0:T(8,128)(2,1)S(1)} async-done(((bf16[64,64,128]{2,1,0:T(8,128)(2,1)}), bf16[64,64,128]{2,1,0:T(8,128)(2,1)S(1)}, u32[]{:S(2)}, u32[]{:S(2)}) %all-to-all-start) | async-done | bytes 1048608 | tf_op jit(solution)/shard_map/all_to_all | solution.py:266
  49.2 0.0 copy-done.4
  49.2 1.9 %predicted_spectra.1 = bf16[256,128]{1,0:T(8,128)(2,1)S(1)} custom-call(s32[1]{0:T(128)} %bitcast.z1_ref, f32[2]{0:T(128)S(1)} %dynamic-slice_reduce_fusion.wave_ref, bf16[16,4,64,128]{3,2,1,0:T(8,128)(2,1)S(1)} %bitcast.8, bf16[512,512]{1,0:T(8,128)(2,1)S(1)} %copy-done.5, bf16[512,512]{1,0:T(8,128)(2,1)S(1)} %copy-done.4), custom_call_target="tpu_custom_call" | custom-call | flops 1073741824 | bytes 2097152 | tf_op jit(solution)/shard_map/predicted_spectra/pallas_call | solution.py:191
  51.1 13.7 %all_to_all.10 = bf16[64,4,128]{2,1,0:T(4,128)(2,1)S(1)} all-to-all(bf16[64,4,128]{2,1,0:T(4,128)(2,1)S(1)} %bitcast.10), channel_id=1, replica_groups=mesh['yh'=2,'z1'=4,'z0'=2,'x'=4,'yl'=2,'core'=2] {'yh','z0','x','yl','co..., dimensions={0} | all-to-all | bytes 131072 | tf_op jit(solution)/shard_map/all_to_all | solution.py:269
  64.8 0.0 copy-done.2
  64.8 1.3 %multiples.1 = bf16[256,2048]{1,0:T(8,128)(2,1)} custom-call(bf16[256,128]{1,0:T(8,128)(2,1)S(1)} %bitcast.9, bf16[128,2048]{1,0:T(8,128)(2,1)S(1)} %copy-done.2), custom_call_target="tpu_custom_call" | custom-call | flops 134217728 | bytes 2097152 | tf_op jit(solution)/shard_map/multiples/pallas_call | solution.py:233
  (3 shorter events, 0.0 us)
Async XLA Ops:
  0.0 32.2 %copy-start = (f32[64,2]{0,1:T(2,128)S(1)}, f32[64,2]{0,1:T(2,128)}, u32[]{:S(2)}) copy-start(f32[64,2]{0,1:T(2,128)} %param.10) | copy-start | bytes 1540
  0.0 14.1 %copy-start.3 = (bf16[2048,128]{1,0:T(8,128)(2,1)S(1)}, bf16[2048,128]{1,0:T(8,128)(2,1)}, u32[]{:S(2)}) copy-start(bf16[2048,128]{1,0:T(8,128)(2,1)} %constant.47.clone.table_hbm.table_ref) | copy-start | bytes 1572868
  0.0 14.1 %copy-start.1 = (bf16[8,256,2048]{2,1,0:T(8,128)(2,1)S(1)}, bf16[8,256,2048]{2,1,0:T(8,128)(2,1)}, u32[]{:S(2)}) copy-start(bf16[8,256,2048]{2,1,0:T(8,128)(2,1)} %x_ref.1) | copy-start | bytes 25165828
  3.1 46.1 %copy-start.4 = (bf16[512,512]{1,0:T(8,128)(2,1)S(1)}, bf16[512,512]{1,0:T(8,128)(2,1)}, u32[]{:S(2)}) copy-start(bf16[512,512]{1,0:T(8,128)(2,1)} %constant.50.clone.back_ref) | copy-start | bytes 1572868
  3.1 46.1 %copy-start.5 = (bf16[512,512]{1,0:T(8,128)(2,1)S(1)}, bf16[512,512]{1,0:T(8,128)(2,1)}, u32[]{:S(2)}) copy-start(bf16[512,512]{1,0:T(8,128)(2,1)} %constant.49.clone.mover_ref) | copy-start | bytes 1572868
  3.2 61.7 %copy-start.2 = (bf16[128,2048]{1,0:T(8,128)(2,1)S(1)}, bf16[128,2048]{1,0:T(8,128)(2,1)}, u32[]{:S(2)}) copy-start(bf16[128,2048]{1,0:T(8,128)(2,1)} %constant.51.clone.table_ref) | copy-start | bytes 1572868
  3.2 15.5 %collective-permute-start.2 = (bf16[512,128]{1,0:T(8,128)(2,1)S(1)}, bf16[512,128]{1,0:T(8,128)(2,1)S(1)}, u32[]{:S(2)}, u32[]{:S(2)}) collective-permute-start(bf16[512,128]{1,0:T(8,128)(2,1)S(1)} %receiver_spectra.1.own_ref), channel_id=1, source_target_pairs={{0,80},{16,64},{32,112},{48,96},{64,16},{80,0},{96,48},{112,32},{1... | collective-permute-start | bytes 393224 | tf_op jit(solution)/shard_map/ppermute | solution.py:262
  10.5 8.1 %collective-permute-start.1 = (bf16[512,128]{1,0:T(8,128)(2,1)S(1)}, bf16[512,128]{1,0:T(8,128)(2,1)S(1)}, u32[]{:S(2)}, u32[]{:S(2)}) collective-permute-start(bf16[512,128]{1,0:T(8,128)(2,1)S(1)} %receiver_spectra.1.own_ref), channel_id=1, source_target_pairs={{0,32},{16,48},{32,64},{48,80},{64,96},{80,112},{96,0},{112,16},{1... | collective-permute-start | bytes 393224 | tf_op jit(solution)/shard_map/ppermute | solution.py:262
  11.7 11.6 %collective-permute-start = (bf16[512,128]{1,0:T(8,128)(2,1)S(1)}, bf16[512,128]{1,0:T(8,128)(2,1)S(1)}, u32[]{:S(2)}, u32[]{:S(2)}) collective-permute-start(bf16[512,128]{1,0:T(8,128)(2,1)S(1)} %receiver_spectra.1.own_ref), channel_id=1, source_target_pairs={{0,96},{16,112},{32,0},{48,16},{64,32},{80,48},{96,64},{112,80},{1... | collective-permute-start | bytes 393224 | tf_op jit(solution)/shard_map/ppermute | solution.py:262
  24.1 25.1 %all-to-all-start = ((bf16[64,64,128]{2,1,0:T(8,128)(2,1)}), bf16[64,64,128]{2,1,0:T(8,128)(2,1)S(1)}, u32[]{:S(2)}, u32[]{:S(2)}) async-start(bf16[64,64,128]{2,1,0:T(8,128)(2,1)} %maximum_dynamic-update-slice_fusion), calls=%async_computation | async-start | bytes 2097152 | tf_op jit(solution)/shard_map/all_to_all | solution.py:266

commit v5 on v4

--- a/solution.py
+++ b/solution.py
@@ -135,13 +135,28 @@
     )(traces, own, table)
 
 
-def product_kernel(z1_ref, wave_ref, got_ref, mover_ref, back_ref, out_ref, right, pred, rows):
+def swapped(tiles):
+    group = lax.broadcasted_iota(jnp.int32, tiles[0].shape, 1) // 32
+    for bit in (1, 2):
+        keep = (group & bit) == 0
+        tiles = list(tiles)
+        for i in range(4):
+            if not i & bit:
+                a, b = tiles[i], tiles[i + bit]
+                tiles[i] = jnp.where(keep, a, pltpu.roll(b, 32 * bit, 1))
+                tiles[i + bit] = jnp.where(keep, pltpu.roll(a, 128 - 32 * bit, 1), b)
+    return tiles
+
+
+def product_kernel(z1_ref, wave_ref, got_ref, out_ref, right, pred, rows):
     z1 = z1_ref[0]
     raw = jnp.zeros((256, 256), jnp.float32)
     for pair in range(2):
         at = 32 + 16 * pair
-        pieces = [got_ref[:, row, at : at + 16, :].reshape(256, 128) for row in range(4)]
-        moved = dot(jnp.concatenate(pieces, axis=1), mover_ref[...]).reshape(2, 8, 2, 8, 512)
+        pieces = [
+            got_ref[:, row, at : at + 16, :].reshape(256, 128).astype(jnp.float32) for row in range(4)
+        ]
+        tiles = [tile.reshape(2, 8, 2, 8, 128) for tile in swapped(pieces)]
         for half in range(2):
             slot = 2 * pair + half
             origin = lax.rem(z1 - SLOTS[slot] + 4, 4)
@@ -150,14 +165,12 @@
                 panel = 2 * yh + lax.div(origin, 2)
                 start = pl.multiple_of(16 * lax.rem(origin, 2), 16)
                 left.append(got_ref[:, panel, pl.ds(start, 16), :].reshape(256, 128))
-                part = moved[yh, :, half]
-                if SLOTS[slot] == 2:
-                    part = jnp.concatenate([part[4:], part[:4]], axis=0)
-                part = part.reshape(64, 512)
                 for k in range(2):
                     for c in range(2):
-                        at = 256 * k + 128 * c
-                        right[slot, c, pl.ds(yh * 128 + k, 64, stride=2), :] = part[:, at : at + 128]
+                        part = tiles[2 * c + k][yh, :, half]
+                        if SLOTS[slot] == 2:
+                            part = jnp.concatenate([part[4:], part[:4]], axis=0)
+                        right[slot, c, pl.ds(yh * 128 + k, 64, stride=2), :] = part.reshape(64, 128)
             coupled = jnp.concatenate([right[slot, 0], right[slot, 1]], axis=1)
             raw += dot(
                 jnp.concatenate(left, axis=1),
@@ -170,20 +183,20 @@
     wave_real, wave_imag = wave_ref[0], wave_ref[1]
     pred[0] = ((real * wave_real - imag * wave_imag) * amplitude).reshape(128, 128)
     pred[1] = ((real * wave_imag + imag * wave_real) * amplitude).reshape(128, 128)
-    wide = []
-    for c in range(2):
-        for high in range(2):
-            wide.append(
-                jnp.concatenate(
-                    [pred[c, pl.ds(high * 4 + low, 16, stride=8), :] for low in range(4)], axis=1
-                )
-            )
-    wide = dot(jnp.concatenate(wide, axis=0).astype(jnp.bfloat16), back_ref[...])
-    for q in range(4):
-        for row in range(4):
-            rows[pl.ds(row * 4 + q, 16, stride=16), :] = wide[
-                q * 16 : (q + 1) * 16, row * 128 : (row + 1) * 128
-            ]
+    wide = [
+        jnp.concatenate(
+            [
+                pred[c, pl.ds(high * 4 + low, 16, stride=8), :]
+                for c in range(2)
+                for high in range(2)
+            ],
+            axis=0,
+        )
+        for low in range(4)
+    ]
+    for row, tile in enumerate(swapped(wide)):
+        for q in range(4):
+            rows[pl.ds(row * 4 + q, 16, stride=16), :] = tile[q * 16 : (q + 1) * 16]
     out_ref[...] = rows[...].astype(jnp.bfloat16)
 
 
@@ -191,7 +204,7 @@
     return pl.pallas_call(
         product_kernel,
         out_shape=jax.ShapeDtypeStruct((256, 128), jnp.bfloat16),
-        in_specs=[SMEM, SMEM] + [VMEM] * 3,
+        in_specs=[SMEM, SMEM, VMEM],
         out_specs=VMEM,
         scratch_shapes=[
             pltpu.VMEM((4, 2, 256, 128), jnp.float32),
@@ -205,8 +218,6 @@
         z1,
         wavelet,
         got.reshape(16, 4, 64, 128),
-        jnp.asarray(mover((4, 2, 2, 32), (2, 1, 0, 3))),
-        jnp.asarray(mover((4, 4, 32), (1, 0, 2))),
     )
 
 

time: 66.3 us -> 65.9 us (level)
  no operation moved by 1% of the time
where the time goes in v5:
time: 65.9 us; the launch traced here: 65.7 us
  waiting for transfers between devices  21.5 us (33%)
  starting transfers between devices  19 us (29%)
  blocking collectives  13.7 us (21%)
  Pallas kernels  10.4 us (16%)
  other arithmetic  0.81 us (1%)
    all_to_all x1, waiting for transfers between devices, per_device(): got = lax.all_to_all(sent, GROUP, split_axis=0, concat_axis=0, tiled=True)  16.8 us
    all_to_all x1, blocking collectives, per_device(): lax.all_to_all(predicted.reshape(NF, 4, 128), GROUP, split_axis=0, concat...  13.7 us
    ppermute x3, starting transfers between devices, per_device(): others = [lax.ppermute(own, ('z1', 'z0'), moves(hop)) for hop in HOPS]  11 us
    all_to_all x1, starting transfers between devices, per_device(): got = lax.all_to_all(sent, GROUP, split_axis=0, concat_axis=0, tiled=True)  8.04 us
    ppermute x3, waiting for transfers between devices, per_device(): others = [lax.ppermute(own, ('z1', 'z0'), moves(hop)) for hop in HOPS]  4.64 us
    pallas_call x1, Pallas kernels, source_spectra(): pl.pallas_call(source_kernel, out_shape=jax.ShapeDtypeStruct((NF, 64, 128...  4.55 us
    pallas_call x1, Pallas kernels, receiver_spectra(): pl.pallas_call(receiver_kernel, out_shape=pltpu.VMEM((NF * 8, 128), jnp.b...  3.11 us
    pallas_call x1, Pallas kernels, predicted_spectra(): pl.pallas_call(product_kernel, out_shape=jax.ShapeDtypeStruct((256, 128),...  1.5 us
  transfers between devices with their start and end apart: 4, of which 2 were waited for; matrix products, arithmetic and copies ran while one was open for 0% of the time, Pallas kernels for 7%

profile of v5, /device:TPU:1, one launch (start us, length us, event | category | flops | bytes accessed | tf_op | source)
XLA Modules:
  0.0 65.7 jit_solution(3233426906771297943)
XLA Ops:
  0.0 0.0 copy-start
  0.0 0.0 copy-start.3
  0.0 0.0 copy-start.1
  0.0 3.1 %receiver_spectra.1.own_ref = bf16[512,128]{1,0:T(8,128)(2,1)S(1)} custom-call(bf16[32,16,2048]{2,1,0:T(8,128)(2,1)} %x_hbm.1, bf16[2048,128]{1,0:T(8,128)(2,1)} %constant.43.clone.table_hbm.table_ref, bf16[512,512]{1,0:T(8,128)(2,1)} %constant.44.clone.mover_hbm), custom_call_target="tpu_custom_call" | custom-call | flops 26843545600 | bytes 3145728 | tf_op jit(solution)/shard_map/receiver_spectra/pallas_call | solution.py:81
  3.1 0.0 copy-start.2
  3.1 7.4 %collective-permute-start.2 = (bf16[512,128]{1,0:T(8,128)(2,1)S(1)}, bf16[512,128]{1,0:T(8,128)(2,1)S(1)}, u32[]{:S(2)}, u32[]{:S(2)}) collective-permute-start(bf16[512,128]{1,0:T(8,128)(2,1)S(1)} %receiver_spectra.1.own_ref), channel_id=1, source_target_pairs={{0,80},{16,64},{32,112},{48,96},{64,16},{80,0},{96,48},{112,32},{1... | collective-permute-start | bytes 393224 | tf_op jit(solution)/shard_map/ppermute | solution.py:273
  10.5 1.2 %collective-permute-start.1 = (bf16[512,128]{1,0:T(8,128)(2,1)S(1)}, bf16[512,128]{1,0:T(8,128)(2,1)S(1)}, u32[]{:S(2)}, u32[]{:S(2)}) collective-permute-start(bf16[512,128]{1,0:T(8,128)(2,1)S(1)} %receiver_spectra.1.own_ref), channel_id=1, source_target_pairs={{0,32},{16,48},{32,64},{48,80},{64,96},{80,112},{96,0},{112,16},{1... | collective-permute-start | bytes 393224 | tf_op jit(solution)/shard_map/ppermute | solution.py:273
  11.7 2.4 %collective-permute-start = (bf16[512,128]{1,0:T(8,128)(2,1)S(1)}, bf16[512,128]{1,0:T(8,128)(2,1)S(1)}, u32[]{:S(2)}, u32[]{:S(2)}) collective-permute-start(bf16[512,128]{1,0:T(8,128)(2,1)S(1)} %receiver_spectra.1.own_ref), channel_id=1, source_target_pairs={{0,96},{16,112},{32,0},{48,16},{64,32},{80,48},{96,64},{112,80},{1... | collective-permute-start | bytes 393224 | tf_op jit(solution)/shard_map/ppermute | solution.py:273
  14.1 0.0 copy-done.3
  14.1 0.0 copy-done.1
  14.1 4.5 %source_spectra.1 = bf16[64,64,128]{2,1,0:T(8,128)(2,1)} custom-call(bf16[8,256,2048]{2,1,0:T(8,128)(2,1)S(1)} %copy-done.1, bf16[512,128]{1,0:T(8,128)(2,1)S(1)} %receiver_spectra.1.own_ref, bf16[2048,128]{1,0:T(8,128)(2,1)S(1)} %copy-done.3), custom_call_target="tpu_custom_call" | custom-call | flops 1073741824 | bytes 10485760 | tf_op jit(solution)/shard_map/source_spectra/pallas_call | solution.py:124
  18.6 0.0 collective-permute-done.2
  18.6 0.0 collective-permute-done.1
  18.7 4.6 %collective-permute-done = bf16[512,128]{1,0:T(8,128)(2,1)S(1)} collective-permute-done((bf16[512,128]{1,0:T(8,128)(2,1)S(1)}, bf16[512,128]{1,0:T(8,128)(2,1)S(1)}, u32[]{:S(2)}, u32[]{:S(2)}) %collective-permute-start) | collective-permute-done | bytes 131104 | tf_op jit(solution)/shard_map/ppermute | solution.py:273
  23.3 0.8 %maximum_dynamic-update-slice_fusion = bf16[64,64,128]{2,1,0:T(8,128)(2,1)} fusion(bf16[64,64,128]{2,1,0:T(8,128)(2,1)} %source_spectra.1, bf16[64,8,128]{2,1,0:T(8,128)(2,1)S(1)} %bitcast.11, bf16[64,8,128]{2,1,0:T(8,128)(2,1)S(1)} %bitcast.12, bf16[64,8,128]{2,1,0:T(8,128)(2,1)S(1)} %bitcast.13), kind=kLoop, calls=%fused_computation | loop fusion | flops 1179648 | bytes 786432 | tf_op jit(solution)/shard_map/dynamic_update_slice | solution.py:276
  24.1 8.0 %all-to-all-start = ((bf16[64,64,128]{2,1,0:T(8,128)(2,1)}), bf16[64,64,128]{2,1,0:T(8,128)(2,1)S(1)}, u32[]{:S(2)}, u32[]{:S(2)}) async-start(bf16[64,64,128]{2,1,0:T(8,128)(2,1)} %maximum_dynamic-update-slice_fusion), calls=%async_computation | async-start | bytes 2097152 | tf_op jit(solution)/shard_map/all_to_all | solution.py:277
  32.2 0.0 copy-done
  32.2 0.2 dynamic-slice_reduce_fusion.wave_ref
  32.4 16.8 %all-to-all-done = bf16[64,64,128]{2,1,0:T(8,128)(2,1)S(1)} async-done(((bf16[64,64,128]{2,1,0:T(8,128)(2,1)}), bf16[64,64,128]{2,1,0:T(8,128)(2,1)S(1)}, u32[]{:S(2)}, u32[]{:S(2)}) %all-to-all-start) | async-done | bytes 1048608 | tf_op jit(solution)/shard_map/all_to_all | solution.py:277
  49.2 1.5 %predicted_spectra.1 = bf16[256,128]{1,0:T(8,128)(2,1)S(1)} custom-call(s32[1]{0:T(128)} %bitcast.z1_ref, f32[2]{0:T(128)S(1)} %dynamic-slice_reduce_fusion.wave_ref, bf16[16,4,64,128]{3,2,1,0:T(8,128)(2,1)S(1)} %bitcast.8), custom_call_target="tpu_custom_call" | custom-call | flops 1073741824 | bytes 2097152 | tf_op jit(solution)/shard_map/predicted_spectra/pallas_call | solution.py:204
  50.7 13.7 %all_to_all.10 = bf16[64,4,128]{2,1,0:T(4,128)(2,1)S(1)} all-to-all(bf16[64,4,128]{2,1,0:T(4,128)(2,1)S(1)} %bitcast.10), channel_id=1, replica_groups=mesh['yh'=2,'z1'=4,'z0'=2,'x'=4,'yl'=2,'core'=2] {'yh','z0','x','yl','co..., dimensions={0} | all-to-all | bytes 131072 | tf_op jit(solution)/shard_map/all_to_all | solution.py:280
  64.4 0.0 copy-done.2
  64.4 1.3 %multiples.1 = bf16[256,2048]{1,0:T(8,128)(2,1)} custom-call(bf16[256,128]{1,0:T(8,128)(2,1)S(1)} %bitcast.9, bf16[128,2048]{1,0:T(8,128)(2,1)S(1)} %copy-done.2), custom_call_target="tpu_custom_call" | custom-call | flops 134217728 | bytes 2097152 | tf_op jit(solution)/shard_map/multiples/pallas_call | solution.py:244
Async XLA Ops:
  0.0 32.2 %copy-start = (f32[64,2]{0,1:T(2,128)S(1)}, f32[64,2]{0,1:T(2,128)}, u32[]{:S(2)}) copy-start(f32[64,2]{0,1:T(2,128)} %param.8) | copy-start | bytes 1540
  0.0 14.1 %copy-start.3 = (bf16[2048,128]{1,0:T(8,128)(2,1)S(1)}, bf16[2048,128]{1,0:T(8,128)(2,1)}, u32[]{:S(2)}) copy-start(bf16[2048,128]{1,0:T(8,128)(2,1)} %constant.43.clone.table_hbm.table_ref) | copy-start | bytes 1572868
  0.0 14.1 %copy-start.1 = (bf16[8,256,2048]{2,1,0:T(8,128)(2,1)S(1)}, bf16[8,256,2048]{2,1,0:T(8,128)(2,1)}, u32[]{:S(2)}) copy-start(bf16[8,256,2048]{2,1,0:T(8,128)(2,1)} %x_ref.1) | copy-start | bytes 25165828
  3.1 61.3 %copy-start.2 = (bf16[128,2048]{1,0:T(8,128)(2,1)S(1)}, bf16[128,2048]{1,0:T(8,128)(2,1)}, u32[]{:S(2)}) copy-start(bf16[128,2048]{1,0:T(8,128)(2,1)} %constant.45.clone.table_ref) | copy-start | bytes 1572868
  3.1 15.5 %collective-permute-start.2 = (bf16[512,128]{1,0:T(8,128)(2,1)S(1)}, bf16[512,128]{1,0:T(8,128)(2,1)S(1)}, u32[]{:S(2)}, u32[]{:S(2)}) collective-permute-start(bf16[512,128]{1,0:T(8,128)(2,1)S(1)} %receiver_spectra.1.own_ref), channel_id=1, source_target_pairs={{0,80},{16,64},{32,112},{48,96},{64,16},{80,0},{96,48},{112,32},{1... | collective-permute-start | bytes 393224 | tf_op jit(solution)/shard_map/ppermute | solution.py:273
  10.5 8.1 %collective-permute-start.1 = (bf16[512,128]{1,0:T(8,128)(2,1)S(1)}, bf16[512,128]{1,0:T(8,128)(2,1)S(1)}, u32[]{:S(2)}, u32[]{:S(2)}) collective-permute-start(bf16[512,128]{1,0:T(8,128)(2,1)S(1)} %receiver_spectra.1.own_ref), channel_id=1, source_target_pairs={{0,32},{16,48},{32,64},{48,80},{64,96},{80,112},{96,0},{112,16},{1... | collective-permute-start | bytes 393224 | tf_op jit(solution)/shard_map/ppermute | solution.py:273
  11.7 11.6 %collective-permute-start = (bf16[512,128]{1,0:T(8,128)(2,1)S(1)}, bf16[512,128]{1,0:T(8,128)(2,1)S(1)}, u32[]{:S(2)}, u32[]{:S(2)}) collective-permute-start(bf16[512,128]{1,0:T(8,128)(2,1)S(1)} %receiver_spectra.1.own_ref), channel_id=1, source_target_pairs={{0,96},{16,112},{32,0},{48,16},{64,32},{80,48},{96,64},{112,80},{1... | collective-permute-start | bytes 393224 | tf_op jit(solution)/shard_map/ppermute | solution.py:273
  24.1 25.1 %all-to-all-start = ((bf16[64,64,128]{2,1,0:T(8,128)(2,1)}), bf16[64,64,128]{2,1,0:T(8,128)(2,1)S(1)}, u32[]{:S(2)}, u32[]{:S(2)}) async-start(bf16[64,64,128]{2,1,0:T(8,128)(2,1)} %maximum_dynamic-update-slice_fusion), calls=%async_computation | async-start | bytes 2097152 | tf_op jit(solution)/shard_map/all_to_all | solution.py:277

commit v6 on v5

--- a/solution.py
+++ b/solution.py
@@ -150,7 +150,7 @@
 
 def product_kernel(z1_ref, wave_ref, got_ref, out_ref, right, pred, rows):
     z1 = z1_ref[0]
-    raw = jnp.zeros((256, 256), jnp.float32)
+    left, coupled = [], []
     for pair in range(2):
         at = 32 + 16 * pair
         pieces = [
@@ -160,7 +160,6 @@
         for half in range(2):
             slot = 2 * pair + half
             origin = lax.rem(z1 - SLOTS[slot] + 4, 4)
-            left = []
             for yh in range(2):
                 panel = 2 * yh + lax.div(origin, 2)
                 start = pl.multiple_of(16 * lax.rem(origin, 2), 16)
@@ -171,11 +170,12 @@
                         if SLOTS[slot] == 2:
                             part = jnp.concatenate([part[4:], part[:4]], axis=0)
                         right[slot, c, pl.ds(yh * 128 + k, 64, stride=2), :] = part.reshape(64, 128)
-            coupled = jnp.concatenate([right[slot, 0], right[slot, 1]], axis=1)
-            raw += dot(
-                jnp.concatenate(left, axis=1),
-                coupled.astype(jnp.bfloat16),
-            )
+            both = jnp.concatenate([right[slot, 0], right[slot, 1]], axis=1)
+            coupled.append(both.astype(jnp.bfloat16))
+    raw = dot(
+        jnp.concatenate(left, axis=1),
+        jnp.concatenate(coupled, axis=0),
+    )
     raw = raw.reshape(16, 2, 8, 256)
     real = raw[:, 0, :, :128] - raw[:, 1, :, 128:]
     imag = raw[:, 0, :, 128:] + raw[:, 1, :, :128]

time: 65.9 us -> 65.9 us (level)
  no operation moved by 1% of the time
where the time goes in v6:
time: 65.9 us; the launch traced here: 65.6 us
  waiting for transfers between devices  21.5 us (33%)
  starting transfers between devices  19 us (29%)
  blocking collectives  13.7 us (21%)
  Pallas kernels  10.4 us (16%)
  other arithmetic  0.81 us (1%)
    all_to_all x1, waiting for transfers between devices, per_device(): got = lax.all_to_all(sent, GROUP, split_axis=0, concat_axis=0, tiled=True)  16.8 us
    all_to_all x1, blocking collectives, per_device(): lax.all_to_all(predicted.reshape(NF, 4, 128), GROUP, split_axis=0, concat...  13.7 us
    ppermute x3, starting transfers between devices, per_device(): others = [lax.ppermute(own, ('z1', 'z0'), moves(hop)) for hop in HOPS]  11 us
    all_to_all x1, starting transfers between devices, per_device(): got = lax.all_to_all(sent, GROUP, split_axis=0, concat_axis=0, tiled=True)  8.04 us
    ppermute x3, waiting for transfers between devices, per_device(): others = [lax.ppermute(own, ('z1', 'z0'), moves(hop)) for hop in HOPS]  4.64 us
    pallas_call x1, Pallas kernels, source_spectra(): pl.pallas_call(source_kernel, out_shape=jax.ShapeDtypeStruct((NF, 64, 128...  4.55 us
    pallas_call x1, Pallas kernels, receiver_spectra(): pl.pallas_call(receiver_kernel, out_shape=pltpu.VMEM((NF * 8, 128), jnp.b...  3.11 us
    pallas_call x1, Pallas kernels, predicted_spectra(): pl.pallas_call(product_kernel, out_shape=jax.ShapeDtypeStruct((256, 128),...  1.5 us
  transfers between devices with their start and end apart: 4, of which 2 were waited for; matrix products, arithmetic and copies ran while one was open for 0% of the time, Pallas kernels for 7%

profile of v6, /device:TPU:1, one launch (start us, length us, event | category | flops | bytes accessed | tf_op | source)
XLA Modules:
  0.0 65.6 jit_solution(2250244716471945234)
XLA Ops:
  0.0 0.0 copy-start
  0.0 0.0 copy-start.3
  0.0 0.0 copy-start.1
  0.0 3.1 %receiver_spectra.1.own_ref = bf16[512,128]{1,0:T(8,128)(2,1)S(1)} custom-call(bf16[32,16,2048]{2,1,0:T(8,128)(2,1)} %x_hbm.1, bf16[2048,128]{1,0:T(8,128)(2,1)} %constant.43.clone.table_hbm.table_ref, bf16[512,512]{1,0:T(8,128)(2,1)} %constant.44.clone.mover_hbm), custom_call_target="tpu_custom_call" | custom-call | flops 26843545600 | bytes 3145728 | tf_op jit(solution)/shard_map/receiver_spectra/pallas_call | solution.py:81
  3.1 0.0 copy-start.2
  3.1 7.4 %collective-permute-start.2 = (bf16[512,128]{1,0:T(8,128)(2,1)S(1)}, bf16[512,128]{1,0:T(8,128)(2,1)S(1)}, u32[]{:S(2)}, u32[]{:S(2)}) collective-permute-start(bf16[512,128]{1,0:T(8,128)(2,1)S(1)} %receiver_spectra.1.own_ref), channel_id=1, source_target_pairs={{0,80},{16,64},{32,112},{48,96},{64,16},{80,0},{96,48},{112,32},{1... | collective-permute-start | bytes 393224 | tf_op jit(solution)/shard_map/ppermute | solution.py:273
  10.5 1.2 %collective-permute-start.1 = (bf16[512,128]{1,0:T(8,128)(2,1)S(1)}, bf16[512,128]{1,0:T(8,128)(2,1)S(1)}, u32[]{:S(2)}, u32[]{:S(2)}) collective-permute-start(bf16[512,128]{1,0:T(8,128)(2,1)S(1)} %receiver_spectra.1.own_ref), channel_id=1, source_target_pairs={{0,32},{16,48},{32,64},{48,80},{64,96},{80,112},{96,0},{112,16},{1... | collective-permute-start | bytes 393224 | tf_op jit(solution)/shard_map/ppermute | solution.py:273
  11.7 2.4 %collective-permute-start = (bf16[512,128]{1,0:T(8,128)(2,1)S(1)}, bf16[512,128]{1,0:T(8,128)(2,1)S(1)}, u32[]{:S(2)}, u32[]{:S(2)}) collective-permute-start(bf16[512,128]{1,0:T(8,128)(2,1)S(1)} %receiver_spectra.1.own_ref), channel_id=1, source_target_pairs={{0,96},{16,112},{32,0},{48,16},{64,32},{80,48},{96,64},{112,80},{1... | collective-permute-start | bytes 393224 | tf_op jit(solution)/shard_map/ppermute | solution.py:273
  14.1 0.0 copy-done.3
  14.1 0.0 copy-done.1
  14.1 4.5 %source_spectra.1 = bf16[64,64,128]{2,1,0:T(8,128)(2,1)} custom-call(bf16[8,256,2048]{2,1,0:T(8,128)(2,1)S(1)} %copy-done.1, bf16[512,128]{1,0:T(8,128)(2,1)S(1)} %receiver_spectra.1.own_ref, bf16[2048,128]{1,0:T(8,128)(2,1)S(1)} %copy-done.3), custom_call_target="tpu_custom_call" | custom-call | flops 1073741824 | bytes 10485760 | tf_op jit(solution)/shard_map/source_spectra/pallas_call | solution.py:124
  18.6 0.0 collective-permute-done.2
  18.6 0.0 collective-permute-done.1
  18.7 4.6 %collective-permute-done = bf16[512,128]{1,0:T(8,128)(2,1)S(1)} collective-permute-done((bf16[512,128]{1,0:T(8,128)(2,1)S(1)}, bf16[512,128]{1,0:T(8,128)(2,1)S(1)}, u32[]{:S(2)}, u32[]{:S(2)}) %collective-permute-start) | collective-permute-done | bytes 131104 | tf_op jit(solution)/shard_map/ppermute | solution.py:273
  23.3 0.8 %maximum_dynamic-update-slice_fusion = bf16[64,64,128]{2,1,0:T(8,128)(2,1)} fusion(bf16[64,64,128]{2,1,0:T(8,128)(2,1)} %source_spectra.1, bf16[64,8,128]{2,1,0:T(8,128)(2,1)S(1)} %bitcast.11, bf16[64,8,128]{2,1,0:T(8,128)(2,1)S(1)} %bitcast.12, bf16[64,8,128]{2,1,0:T(8,128)(2,1)S(1)} %bitcast.13), kind=kLoop, calls=%fused_computation | loop fusion | flops 1179648 | bytes 786432 | tf_op jit(solution)/shard_map/dynamic_update_slice | solution.py:276
  24.1 8.0 %all-to-all-start = ((bf16[64,64,128]{2,1,0:T(8,128)(2,1)}), bf16[64,64,128]{2,1,0:T(8,128)(2,1)S(1)}, u32[]{:S(2)}, u32[]{:S(2)}) async-start(bf16[64,64,128]{2,1,0:T(8,128)(2,1)} %maximum_dynamic-update-slice_fusion), calls=%async_computation | async-start | bytes 2097152 | tf_op jit(solution)/shard_map/all_to_all | solution.py:277
  32.2 0.0 copy-done
  32.2 0.2 dynamic-slice_reduce_fusion.wave_ref
  32.4 16.8 %all-to-all-done = bf16[64,64,128]{2,1,0:T(8,128)(2,1)S(1)} async-done(((bf16[64,64,128]{2,1,0:T(8,128)(2,1)}), bf16[64,64,128]{2,1,0:T(8,128)(2,1)S(1)}, u32[]{:S(2)}, u32[]{:S(2)}) %all-to-all-start) | async-done | bytes 1048608 | tf_op jit(solution)/shard_map/all_to_all | solution.py:277
  49.2 1.5 %predicted_spectra.1 = bf16[256,128]{1,0:T(8,128)(2,1)S(1)} custom-call(s32[1]{0:T(128)} %bitcast.z1_ref, f32[2]{0:T(128)S(1)} %dynamic-slice_reduce_fusion.wave_ref, bf16[16,4,64,128]{3,2,1,0:T(8,128)(2,1)S(1)} %bitcast.8), custom_call_target="tpu_custom_call" | custom-call | flops 1073741824 | bytes 2097152 | tf_op jit(solution)/shard_map/predicted_spectra/pallas_call | solution.py:204
  50.7 13.7 %all_to_all.10 = bf16[64,4,128]{2,1,0:T(4,128)(2,1)S(1)} all-to-all(bf16[64,4,128]{2,1,0:T(4,128)(2,1)S(1)} %bitcast.10), channel_id=1, replica_groups=mesh['yh'=2,'z1'=4,'z0'=2,'x'=4,'yl'=2,'core'=2] {'yh','z0','x','yl','co..., dimensions={0} | all-to-all | bytes 131072 | tf_op jit(solution)/shard_map/all_to_all | solution.py:280
  64.4 0.0 copy-done.2
  64.4 1.3 %multiples.1 = bf16[256,2048]{1,0:T(8,128)(2,1)} custom-call(bf16[256,128]{1,0:T(8,128)(2,1)S(1)} %bitcast.9, bf16[128,2048]{1,0:T(8,128)(2,1)S(1)} %copy-done.2), custom_call_target="tpu_custom_call" | custom-call | flops 134217728 | bytes 2097152 | tf_op jit(solution)/shard_map/multiples/pallas_call | solution.py:244
Async XLA Ops:
  0.0 32.2 %copy-start = (f32[64,2]{0,1:T(2,128)S(1)}, f32[64,2]{0,1:T(2,128)}, u32[]{:S(2)}) copy-start(f32[64,2]{0,1:T(2,128)} %param.8) | copy-start | bytes 1540
  0.0 14.1 %copy-start.3 = (bf16[2048,128]{1,0:T(8,128)(2,1)S(1)}, bf16[2048,128]{1,0:T(8,128)(2,1)}, u32[]{:S(2)}) copy-start(bf16[2048,128]{1,0:T(8,128)(2,1)} %constant.43.clone.table_hbm.table_ref) | copy-start | bytes 1572868
  0.0 14.1 %copy-start.1 = (bf16[8,256,2048]{2,1,0:T(8,128)(2,1)S(1)}, bf16[8,256,2048]{2,1,0:T(8,128)(2,1)}, u32[]{:S(2)}) copy-start(bf16[8,256,2048]{2,1,0:T(8,128)(2,1)} %x_ref.1) | copy-start | bytes 25165828
  3.1 61.3 %copy-start.2 = (bf16[128,2048]{1,0:T(8,128)(2,1)S(1)}, bf16[128,2048]{1,0:T(8,128)(2,1)}, u32[]{:S(2)}) copy-start(bf16[128,2048]{1,0:T(8,128)(2,1)} %constant.45.clone.table_ref) | copy-start | bytes 1572868
  3.1 15.5 %collective-permute-start.2 = (bf16[512,128]{1,0:T(8,128)(2,1)S(1)}, bf16[512,128]{1,0:T(8,128)(2,1)S(1)}, u32[]{:S(2)}, u32[]{:S(2)}) collective-permute-start(bf16[512,128]{1,0:T(8,128)(2,1)S(1)} %receiver_spectra.1.own_ref), channel_id=1, source_target_pairs={{0,80},{16,64},{32,112},{48,96},{64,16},{80,0},{96,48},{112,32},{1... | collective-permute-start | bytes 393224 | tf_op jit(solution)/shard_map/ppermute | solution.py:273
  10.5 8.1 %collective-permute-start.1 = (bf16[512,128]{1,0:T(8,128)(2,1)S(1)}, bf16[512,128]{1,0:T(8,128)(2,1)S(1)}, u32[]{:S(2)}, u32[]{:S(2)}) collective-permute-start(bf16[512,128]{1,0:T(8,128)(2,1)S(1)} %receiver_spectra.1.own_ref), channel_id=1, source_target_pairs={{0,32},{16,48},{32,64},{48,80},{64,96},{80,112},{96,0},{112,16},{1... | collective-permute-start | bytes 393224 | tf_op jit(solution)/shard_map/ppermute | solution.py:273
  11.7 11.6 %collective-permute-start = (bf16[512,128]{1,0:T(8,128)(2,1)S(1)}, bf16[512,128]{1,0:T(8,128)(2,1)S(1)}, u32[]{:S(2)}, u32[]{:S(2)}) collective-permute-start(bf16[512,128]{1,0:T(8,128)(2,1)S(1)} %receiver_spectra.1.own_ref), channel_id=1, source_target_pairs={{0,96},{16,112},{32,0},{48,16},{64,32},{80,48},{96,64},{112,80},{1... | collective-permute-start | bytes 393224 | tf_op jit(solution)/shard_map/ppermute | solution.py:273
  24.1 25.1 %all-to-all-start = ((bf16[64,64,128]{2,1,0:T(8,128)(2,1)}), bf16[64,64,128]{2,1,0:T(8,128)(2,1)S(1)}, u32[]{:S(2)}, u32[]{:S(2)}) async-start(bf16[64,64,128]{2,1,0:T(8,128)(2,1)} %maximum_dynamic-update-slice_fusion), calls=%async_computation | async-start | bytes 2097152 | tf_op jit(solution)/shard_map/all_to_all | solution.py:277
